TPU v7x, 32 devices: a whole 2x2x4 slice. The times are simulated.
32 devices in a mesh: dp: 2 (over y), tm: 8 (over z, core), height: 2 (over x).
Axes of the slice: x: 2, y: 2, z: 4, core: 2. Of those that a mesh axis runs over, the one named last changes fastest.
Arguments:
- clip_input: bfloat16 [2, 32, 8, 96, 128], P('dp', 'tm', 'height'), may hold values from -6 to 6
- cotangent: bfloat16 [2, 32, 8, 96, 128], P('dp', 'tm', 'height'), may hold values from -6 to 6
- first_kernel: bfloat16 [2592, 96], replicated, may hold values from -0.125 to 0.125
- second_kernel: bfloat16 [2592, 96], replicated, may hold values from -0.125 to 0.125
Outputs:
- block_output: float32 [2, 32, 8, 96, 128], P('dp', 'tm', 'height')
- input_grad: float32 [2, 32, 8, 96, 128], P('dp', 'tm', 'height')
- first_grad: float32 [2592, 96], P('dp')
- second_grad: float32 [2592, 96], P('dp')
All inputs are finite; a program needn't handle non-finite values.
Results may differ from a plain program's by a relative error of at most 0.0048.
Values may be sent and summed in bfloat16 or wider, within the bound.
A program may use at most 64 MiB of HBM per device.

v0:
```python
import math

import jax
import jax.numpy as jnp
from jax import lax
from jax.sharding import PartitionSpec as P

EPSILON = 1e-06


def extended_2(array, sides, width):
    for axis, dim in sides:
        peers, length = (lax.axis_size(axis), array.shape[dim])
        up = [(i, (i + 1) % peers) for i in range(peers - 1)]
        down = [(j, i) for i, j in up]
        last = lax.slice_in_dim(array, length - width, length, axis=dim)
        first = lax.slice_in_dim(array, 0, width, axis=dim)
        before = lax.ppermute(last, axis, up)
        after = lax.ppermute(first, axis, down)
        array = jnp.concatenate([before, array, after], axis=dim)
    return array


def passed_along(array, axis, by):
    peers = lax.axis_size(axis)
    pairs = [(i, i + by) for i in range(peers) if 0 <= i + by < peers]
    return lax.ppermute(array, axis, pairs)


def norm_silu(field):
    factor = lax.rsqrt(jnp.mean(field * field, axis=2, keepdims=True) + EPSILON)
    return jax.nn.silu(field * factor)


def pad_rows(extended):
    rimmed = extended_2(extended, (("height", 1),), 1)
    return jnp.pad(rimmed, ((0, 0), (0, 0), (0, 0), (1, 1)))


def time_stack(padded, tap_row, tap_col, frames):
    row_count = padded.shape[1] - 2
    col_count = padded.shape[3] - 2
    window = padded[:, tap_row : tap_row + row_count, :, tap_col : tap_col + col_count]
    return jnp.concatenate([window[offset : offset + frames] for offset in range(3)], axis=2)


def local_conv(padded, kernel, frames):
    channels = padded.shape[2]
    summed = None
    for tap_row in range(3):
        for tap_col in range(3):
            stacked = time_stack(padded, tap_row, tap_col, frames)
            weight = kernel[:, tap_row, tap_col].reshape(3 * channels, kernel.shape[4])
            partial_sum = jnp.einsum(
                "frkw,kd->frdw", stacked, weight, preferred_element_type=jnp.float32
            )
            summed = partial_sum if summed is None else summed + partial_sum
    return summed


def kernel_grad(padded, grad_out, frames):
    channels = padded.shape[2]
    row_list = []
    for tap_row in range(3):
        col_list = []
        for tap_col in range(3):
            stacked = time_stack(padded, tap_row, tap_col, frames)
            piece = jnp.einsum(
                "frkw,frdw->kd", stacked, grad_out, preferred_element_type=jnp.float32
            )
            col_list.append(piece.reshape(3, channels, grad_out.shape[2]))
        row_list.append(jnp.stack(col_list, axis=1))
    gathered = jnp.stack(row_list, axis=1)
    return gathered.reshape(27 * channels, grad_out.shape[2])


def flipped(kernel):
    return jnp.swapaxes(kernel[::-1, ::-1, ::-1], 3, 4)


def local(clip_input, cotangent, first_kernel, second_kernel):
    frames = clip_input.shape[1]
    channels = clip_input.shape[3]
    source = clip_input[0]
    upstream = cotangent[0]
    kernel_one = first_kernel.reshape(3, 3, 3, channels, channels)
    kernel_two = second_kernel.reshape(3, 3, 3, channels, channels)

    def extend_back(block):
        earlier = passed_along(block[frames - 2 :], "tm", 1)
        return pad_rows(jnp.concatenate([earlier, block], axis=0))

    def extend_ahead(block):
        later = passed_along(block[:2], "tm", -1)
        return pad_rows(jnp.concatenate([block, later], axis=0))

    source_float = source.astype(jnp.float32)
    first_act = norm_silu(source_float).astype(jnp.bfloat16)
    first_padded = extend_back(first_act)
    middle = local_conv(first_padded, kernel_one, frames)
    second_act = norm_silu(middle).astype(jnp.bfloat16)
    second_padded = extend_back(second_act)
    branch = local_conv(second_padded, kernel_two, frames)
    block_output = source_float + branch
    second_back = local_conv(extend_ahead(upstream), flipped(kernel_two), frames)
    unused, pull_mid = jax.vjp(norm_silu, middle)
    middle_grad = pull_mid(second_back)[0].astype(jnp.bfloat16)
    first_back = local_conv(extend_ahead(middle_grad), flipped(kernel_one), frames)
    unused, pull_src = jax.vjp(norm_silu, source_float)
    input_grad = upstream.astype(jnp.float32) + pull_src(first_back)[0]
    positions = (
        frames
        * source.shape[1]
        * source.shape[3]
        * lax.axis_size("dp")
        * lax.axis_size("tm")
        * lax.axis_size("height")
    )
    factor = 1.0 / math.sqrt(positions)
    first_term = kernel_grad(first_padded, middle_grad, frames) * factor
    second_term = kernel_grad(second_padded, upstream, frames) * factor
    first_whole, second_whole = lax.psum((first_term, second_term), ("tm", "height"))
    first_grad, second_grad = (
        lax.psum_scatter(first_whole, "dp", scatter_dimension=0, tiled=True),
        lax.psum_scatter(second_whole, "dp", scatter_dimension=0, tiled=True),
    )
    return (block_output[None], input_grad[None], first_grad, second_grad)


def solution(mesh):
    return jax.shard_map(
        local,
        mesh=mesh,
        in_specs=(
            P("dp", "tm", "height", None, None),
            P("dp", "tm", "height", None, None),
            P(),
            P(),
        ),
        out_specs=(
            P("dp", "tm", "height", None, None),
            P("dp", "tm", "height", None, None),
            P("dp", None),
            P("dp", None),
        ),
        check_vma=False,
    )
```

profile of v0, /device:TPU:0, one launch (start us, length us, event | category | flops | bytes accessed | tf_op | source)
XLA Modules:
  0.0 240.6 jit_solution(6959624439068643985)
XLA Ops:
  7.2 1.0 slice_bitcast_fusion
  8.2 1.3 collective-permute-start.6
  9.5 1.1 fusion.132
  10.6 1.2 fusion.124
  11.9 3.2 %collective-permute-start = (bf16[2,4,96,128]{3,2,1,0:T(8,128)(2,1)S(1)}, bf16[2,4,96,128]{3,2,1,0:T(8,128)(2,1)S(1)}, u32[]{:S(2)}, u32[]{:S(2)}) collective-permute-start(bf16[2,4,96,128]{3,2,1,0:T(8,128)(2,1)S(1)} %slice.856), channel_id=1, source_target_pairs={{0,2},{2,4},{4,6},{6,8},{8,10},{10,12},{12,14},{1,3},{3,5},{5,7},{... | collective-permute-start | bytes 589832 | tf_op jit(solution)/shard_map/ppermute | solution.py:27
  15.4 0.8 fusion.225
  16.7 0.9 fusion.224
  17.6 0.7 copy.91
  18.4 0.7 copy.89
  19.1 0.7 copy.87
  19.8 0.7 copy.85
  20.6 0.7 copy.83
  21.3 0.7 copy.81
  22.0 0.7 copy.79
  22.8 0.7 copy.77
  23.5 0.8 copy.75
  25.4 4.9 %collective-permute-start.7 = (bf16[6,1,96,128]{3,2,1,0:T(8,128)(2,1)S(1)}, bf16[6,1,96,128]{3,2,1,0:T(8,128)(2,1)S(1)}, u32[]{:S(2)}, u32[]{:S(2)}) collective-permute-start(bf16[6,1,96,128]{3,2,1,0:T(8,128)(2,1)S(1)} %get-tuple-element.150), channel_id=1, source_target_pairs={{0,1},{2,3},{4,5},{6,7},{8,9},{10,11},{12,13},{14,15},{16,17},{18,... | collective-permute-start | bytes 442376 | tf_op jit(solution)/shard_map/ppermute | solution.py:18
  30.3 1.3 collective-permute-start.8
  31.6 1.3 collective-permute-start.2
  32.9 4.6 %collective-permute-start.1 = (bf16[6,1,96,128]{3,2,1,0:T(8,128)(2,1)S(1)}, bf16[6,1,96,128]{3,2,1,0:T(8,128)(2,1)S(1)}, u32[]{:S(2)}, u32[]{:S(2)}) collective-permute-start(bf16[6,1,96,128]{3,2,1,0:T(8,128)(2,1)S(1)} %get-tuple-element.159), channel_id=1, source_target_pairs={{0,1},{2,3},{4,5},{6,7},{8,9},{10,11},{12,13},{14,15},{16,17},{18,... | collective-permute-start | bytes 442376 | tf_op jit(solution)/shard_map/ppermute | solution.py:18
  37.6 1.3 collective-permute-done.8
  38.9 1.0 select_maximum_fusion.3
  39.9 2.0 fusion.211
  42.0 1.0 fusion.8
  43.0 2.1 fusion.213
  52.8 0.5 multiply_reduce_fusion.1
  57.5 0.7 multiply_reduce_fusion
  62.3 1.3 collective-permute-start.9
  63.6 3.0 %collective-permute-start.3 = (bf16[2,4,96,128]{3,2,1,0:T(8,128)(2,1)S(1)}, bf16[2,4,96,128]{3,2,1,0:T(8,128)(2,1)S(1)}, u32[]{:S(2)}, u32[]{:S(2)}) collective-permute-start(bf16[2,4,96,128]{3,2,1,0:T(8,128)(2,1)S(1)} %slice.896), channel_id=1, source_target_pairs={{0,2},{2,4},{4,6},{6,8},{8,10},{10,12},{12,14},{1,3},{3,5},{5,7},{... | collective-permute-start | bytes 589832 | tf_op jit(solution)/shard_map/ppermute | solution.py:27
  67.4 1.2 copy.93
  68.7 1.3 collective-permute-start.5
  70.0 4.6 %collective-permute-start.4 = (bf16[6,1,96,128]{3,2,1,0:T(8,128)(2,1)S(1)}, bf16[6,1,96,128]{3,2,1,0:T(8,128)(2,1)S(1)}, u32[]{:S(2)}, u32[]{:S(2)}) collective-permute-start(bf16[6,1,96,128]{3,2,1,0:T(8,128)(2,1)S(1)} %get-tuple-element.155), channel_id=1, source_target_pairs={{0,1},{2,3},{4,5},{6,7},{8,9},{10,11},{12,13},{14,15},{16,17},{18,... | collective-permute-start | bytes 442376 | tf_op jit(solution)/shard_map/ppermute | solution.py:18
  74.7 1.3 collective-permute-start.10
  76.0 1.5 collective-permute-start.11
  78.1 0.8 fusion.147
  81.0 1.0 select_maximum_fusion.6
  81.9 2.0 fusion.212
  84.0 0.5 convolution_bitcast_fusion
  84.5 0.5 convolution_bitcast_fusion.2
  85.1 0.5 convolution_bitcast_fusion.3
  85.6 0.5 convolution_bitcast_fusion.5
  86.2 0.5 convolution_bitcast_fusion.6
  86.7 0.5 convolution_bitcast_fusion.8
  87.5 1.2 copy.103
  93.7 0.7 copy-done.31
  94.9 0.5 copy-done.1
  95.5 1.3 fusion.16
  96.8 1.1 fusion.214
  97.9 1.1 fusion.215
  99.0 1.0 select_maximum_fusion
  100.0 3.1 %fusion.210 = (bf16[4,4,96,128]{3,2,1,0:T(8,128)(2,1)S(1)}, bf16[4,4,96,128]{3,2,1,0:T(8,128)(2,1)S(1)}, bf16[4,4,96,128]{3,2,1,0:T(8,128)(2,1)S(1)}, bf16[4,4,9...) fusion(bf16[6,6,96,130]{3,2,1,0:T(8,128)(2,1)S(1)} %select_maxi, ...), kind=kLoop, calls=%fused_computation.330 | loop fusion | bytes 14155776 | tf_op jit(solution)/shard_map/slice | solution.py:44
  103.5 1.8 fusion.78
  105.8 0.5 copy-done.11
  107.0 0.5 copy-done.8
  108.2 0.5 copy-done.5
  109.5 0.5 copy-done.20
  110.5 0.5 copy-done.4
  111.5 0.5 copy-done.17
  113.1 0.7 fusion.133
  113.9 17.9 %reduce-scatter.5.cloned.1.call-done = f32[1296,96]{1,0:T(8,128)} async-done(((f32[2592,96]{1,0:T(8,128)}), f32[1296,96]{1,0:T(8,128)}) %reduce-scatter.5.cloned.1.call-update) | async-done | bytes 497680 | tf_op jit(solution)/shard_map/reduce_scatter | solution.py:125
  131.8 1.1 fusion.131
  132.9 96.8 %all-reduce.7.cloned.1.call-done = (f32[1296,96]{1,0:T(8,128)}, f32[1296,96]{1,0:T(8,128)}) async-done(((f32[1296,96]{1,0:T(8,128)}, f32[1296,96]{1,0:T(8,128)}), (f32[1296,96]{1,0:T(8,128)}, f32[1296,96]{1,0:T(8,128)})) %all-reduce.7.cloned.1.call-update) | async-done | bytes 995344 | tf_op jit(solution)/shard_map/psum | solution.py:122
  229.8 2.1 copy.104
  231.9 2.1 copy.105
  (202 shorter events, 32.6 us)
Async XLA Ops:
  7.2 7.9 %copy-start.2 = (bf16[2592,96]{0,1:T(8,128)(2,1)S(1)}, bf16[2592,96]{0,1:T(8,128)(2,1)}, u32[]{:S(2)}) copy-start(bf16[2592,96]{0,1:T(8,128)(2,1)} %param.6) | copy-start | bytes 1492996
  7.2 106.7 %reduce-scatter.3.cloned.1.call-start = ((), (), s32[]{:S(2)}) async-start(), calls=%async_computation.2 | async-start | bytes 1990656 | tf_op jit(solution)/shard_map/reduce_scatter | solution.py:124
  8.2 17.1 %collective-permute-start.6 = (bf16[2,4,96,128]{3,2,1,0:T(8,128)(2,1)S(1)}, bf16[2,4,96,128]{3,2,1,0:T(8,128)(2,1)S(1)}, u32[]{:S(2)}, u32[]{:S(2)}) collective-permute-start(bf16[2,4,96,128]{3,2,1,0:T(8,128)(2,1)S(1)} %slice_bitcast_fusion), channel_id=1, source_target_pairs={{2,0},{4,2},{6,4},{8,6},{10,8},{12,10},{14,12},{3,1},{5,3},{7,5},{... | collective-permute-start | bytes 589832 | tf_op jit(solution)/shard_map/ppermute | solution.py:27
  11.9 4.4 %copy-start.3 = (bf16[2592,96]{0,1:T(8,128)(2,1)S(1)}, bf16[2592,96]{0,1:T(8,128)(2,1)}, u32[]{:S(2)}) copy-start(bf16[2592,96]{0,1:T(8,128)(2,1)} %param.7) | copy-start | bytes 1492996
  11.9 19.7 %collective-permute-start = (bf16[2,4,96,128]{3,2,1,0:T(8,128)(2,1)S(1)}, bf16[2,4,96,128]{3,2,1,0:T(8,128)(2,1)S(1)}, u32[]{:S(2)}, u32[]{:S(2)}) collective-permute-start(bf16[2,4,96,128]{3,2,1,0:T(8,128)(2,1)S(1)} %slice.856), channel_id=1, source_target_pairs={{0,2},{2,4},{4,6},{6,8},{8,10},{10,12},{12,14},{1,3},{3,5},{5,7},{... | collective-permute-start | bytes 589832 | tf_op jit(solution)/shard_map/ppermute | solution.py:27
  17.6 7.8 %copy-start = (bf16[1,4,4,96,128]{4,3,2,1,0:T(8,128)(2,1)S(1)}, bf16[1,4,4,96,128]{4,3,2,1,0:T(8,128)(2,1)}, u32[]{:S(2)}) copy-start(bf16[1,4,4,96,128]{4,3,2,1,0:T(8,128)(2,1)} %param.5) | copy-start | bytes 1179652
  25.4 12.2 %collective-permute-start.7 = (bf16[6,1,96,128]{3,2,1,0:T(8,128)(2,1)S(1)}, bf16[6,1,96,128]{3,2,1,0:T(8,128)(2,1)S(1)}, u32[]{:S(2)}, u32[]{:S(2)}) collective-permute-start(bf16[6,1,96,128]{3,2,1,0:T(8,128)(2,1)S(1)} %get-tuple-element.150), channel_id=1, source_target_pairs={{0,1},{2,3},{4,5},{6,7},{8,9},{10,11},{12,13},{14,15},{16,17},{18,... | collective-permute-start | bytes 442376 | tf_op jit(solution)/shard_map/ppermute | solution.py:18
  30.3 8.6 %collective-permute-start.8 = (bf16[6,1,96,128]{3,2,1,0:T(8,128)(2,1)S(1)}, bf16[6,1,96,128]{3,2,1,0:T(8,128)(2,1)S(1)}, u32[]{:S(2)}, u32[]{:S(2)}) collective-permute-start(bf16[6,1,96,128]{3,2,1,0:T(8,128)(2,1)S(1)} %get-tuple-element.151), channel_id=1, source_target_pairs={{1,0},{3,2},{5,4},{7,6},{9,8},{11,10},{13,12},{15,14},{17,16},{19,... | collective-permute-start | bytes 442376 | tf_op jit(solution)/shard_map/ppermute | solution.py:19
  31.6 10.4 %collective-permute-start.2 = (bf16[6,1,96,128]{3,2,1,0:T(8,128)(2,1)S(1)}, bf16[6,1,96,128]{3,2,1,0:T(8,128)(2,1)S(1)}, u32[]{:S(2)}, u32[]{:S(2)}) collective-permute-start(bf16[6,1,96,128]{3,2,1,0:T(8,128)(2,1)S(1)} %get-tuple-element.158), channel_id=1, source_target_pairs={{1,0},{3,2},{5,4},{7,6},{9,8},{11,10},{13,12},{15,14},{17,16},{19,... | collective-permute-start | bytes 442376 | tf_op jit(solution)/shard_map/ppermute | solution.py:19
  32.9 9.1 %collective-permute-start.1 = (bf16[6,1,96,128]{3,2,1,0:T(8,128)(2,1)S(1)}, bf16[6,1,96,128]{3,2,1,0:T(8,128)(2,1)S(1)}, u32[]{:S(2)}, u32[]{:S(2)}) collective-permute-start(bf16[6,1,96,128]{3,2,1,0:T(8,128)(2,1)S(1)} %get-tuple-element.159), channel_id=1, source_target_pairs={{0,1},{2,3},{4,5},{6,7},{8,9},{10,11},{12,13},{14,15},{16,17},{18,... | collective-permute-start | bytes 442376 | tf_op jit(solution)/shard_map/ppermute | solution.py:18
  45.2 0.9 copy-start.46
  45.7 0.9 copy-start.45
  46.6 0.9 copy-start.44
  47.5 0.9 copy-start.43
  48.4 0.9 copy-start.42
  49.2 0.9 copy-start.41
  50.1 0.9 copy-start.40
  51.0 0.9 copy-start.39
  51.9 0.9 copy-start.38
  62.3 12.3 %collective-permute-start.9 = (bf16[2,4,96,128]{3,2,1,0:T(8,128)(2,1)S(1)}, bf16[2,4,96,128]{3,2,1,0:T(8,128)(2,1)S(1)}, u32[]{:S(2)}, u32[]{:S(2)}) collective-permute-start(bf16[2,4,96,128]{3,2,1,0:T(8,128)(2,1)S(1)} %slice.975), channel_id=1, source_target_pairs={{2,0},{4,2},{6,4},{8,6},{10,8},{12,10},{14,12},{3,1},{5,3},{7,5},{... | collective-permute-start | bytes 589832 | tf_op jit(solution)/shard_map/ppermute | solution.py:27
  63.6 5.1 %collective-permute-start.3 = (bf16[2,4,96,128]{3,2,1,0:T(8,128)(2,1)S(1)}, bf16[2,4,96,128]{3,2,1,0:T(8,128)(2,1)S(1)}, u32[]{:S(2)}, u32[]{:S(2)}) collective-permute-start(bf16[2,4,96,128]{3,2,1,0:T(8,128)(2,1)S(1)} %slice.896), channel_id=1, source_target_pairs={{0,2},{2,4},{4,6},{6,8},{8,10},{10,12},{12,14},{1,3},{3,5},{5,7},{... | collective-permute-start | bytes 589832 | tf_op jit(solution)/shard_map/ppermute | solution.py:27
  68.6 63.1 %reduce-scatter.5.cloned.1.call-start = ((), (), s32[]{:S(2)}) async-start(), calls=%async_computation.3 | async-start | bytes 1990656 | tf_op jit(solution)/shard_map/reduce_scatter | solution.py:125
  68.7 10.2 %collective-permute-start.5 = (bf16[6,1,96,128]{3,2,1,0:T(8,128)(2,1)S(1)}, bf16[6,1,96,128]{3,2,1,0:T(8,128)(2,1)S(1)}, u32[]{:S(2)}, u32[]{:S(2)}) collective-permute-start(bf16[6,1,96,128]{3,2,1,0:T(8,128)(2,1)S(1)} %get-tuple-element.154), channel_id=1, source_target_pairs={{1,0},{3,2},{5,4},{7,6},{9,8},{11,10},{13,12},{15,14},{17,16},{19,... | collective-permute-start | bytes 442376 | tf_op jit(solution)/shard_map/ppermute | solution.py:19
  70.0 8.9 %collective-permute-start.4 = (bf16[6,1,96,128]{3,2,1,0:T(8,128)(2,1)S(1)}, bf16[6,1,96,128]{3,2,1,0:T(8,128)(2,1)S(1)}, u32[]{:S(2)}, u32[]{:S(2)}) collective-permute-start(bf16[6,1,96,128]{3,2,1,0:T(8,128)(2,1)S(1)} %get-tuple-element.155), channel_id=1, source_target_pairs={{0,1},{2,3},{4,5},{6,7},{8,9},{10,11},{12,13},{14,15},{16,17},{18,... | collective-permute-start | bytes 442376 | tf_op jit(solution)/shard_map/ppermute | solution.py:18
  74.7 18.9 %collective-permute-start.10 = (bf16[6,1,96,128]{3,2,1,0:T(8,128)(2,1)S(1)}, bf16[6,1,96,128]{3,2,1,0:T(8,128)(2,1)S(1)}, u32[]{:S(2)}, u32[]{:S(2)}) collective-permute-start(bf16[6,1,96,128]{3,2,1,0:T(8,128)(2,1)S(1)} %get-tuple-element.146), channel_id=1, source_target_pairs={{0,1},{2,3},{4,5},{6,7},{8,9},{10,11},{12,13},{14,15},{16,17},{18,... | collective-permute-start | bytes 442376 | tf_op jit(solution)/shard_map/ppermute | solution.py:18
  76.0 17.7 %collective-permute-start.11 = (bf16[6,1,96,128]{3,2,1,0:T(8,128)(2,1)S(1)}, bf16[6,1,96,128]{3,2,1,0:T(8,128)(2,1)S(1)}, u32[]{:S(2)}, u32[]{:S(2)}) collective-permute-start(bf16[6,1,96,128]{3,2,1,0:T(8,128)(2,1)S(1)} %get-tuple-element.147), channel_id=1, source_target_pairs={{1,0},{3,2},{5,4},{7,6},{9,8},{11,10},{13,12},{15,14},{17,16},{19,... | collective-permute-start | bytes 442376 | tf_op jit(solution)/shard_map/ppermute | solution.py:19
  87.5 1.2 copy-start.37
  88.7 0.9 copy-start.36
  89.6 0.9 copy-start.35
  90.5 0.9 copy-start.34
  91.4 0.9 copy-start.33
  92.3 0.9 copy-start.32
  93.6 0.9 copy-start.31
  94.5 1.0 copy-start.1
  94.5 1.0 copy-start.30
  100.0 3.5 %copy-start.29 = (bf16[3,1,1,96,96]{4,3,0,2,1:T(8,128)(2,1)S(1)}, bf16[3,1,1,96,96]{4,3,0,2,1:T(8,128)(2,1)}, u32[]{:S(2)}) copy-start(bf16[3,1,1,96,96]{4,3,0,2,1:T(8,128)(2,1)} %copy.77) | copy-start | bytes 165892
  103.1 2.2 copy-start.27
  103.1 126.6 %all-reduce.7.cloned.1.call-start = ((), (), s32[]{:S(2)}) async-start(), calls=%async_computation.4 | async-start | bytes 2654208 | tf_op jit(solution)/shard_map/psum | solution.py:122
  103.4 1.9 copy-start.14
  103.5 1.9 copy-start.15
  103.5 1.9 copy-start.16
  105.3 1.0 copy-start.11
  105.3 1.1 copy-start.12
  105.3 1.2 copy-start.13
  105.3 1.2 copy-start.28
  106.5 1.0 copy-start.8
  106.5 1.1 copy-start.9
  106.5 1.2 copy-start.10
  106.5 1.2 copy-start.26
  107.8 1.0 copy-start.5
  107.8 1.1 copy-start.6
  107.8 1.2 copy-start.7
  107.8 1.2 copy-start.25
  109.0 1.0 copy-start.20
  109.0 1.0 copy-start.24
  110.0 1.0 copy-start.4
  110.0 1.0 copy-start.23
  111.0 1.0 copy-start.17
  111.0 1.1 copy-start.18
  111.0 1.2 copy-start.19
  111.0 1.2 copy-start.22
  112.2 0.9 copy-start.21
Sparse Core Ops, SparseCore 0:
  68.8 24.7 reduce-scatter.2
  103.2 28.5 reduce-scatter.4
  135.4 94.3 all-reduce.6
where the time goes:
time: 242 us; the launch traced here: 241 us
  waiting for transfers between devices  116 us (48%)
  local copies, waits for them, and re-layouts  41.9 us (17%)
  starting transfers between devices  29.9 us (12%)
  matrix products  27.2 us (11%)
  between operations  15 us (6%)
  other arithmetic  10.3 us (4%)
    psum x1, waiting for transfers between devices, local(): lax.psum((first_term, second_term), ('tm', 'height'))  96.8 us
    dot_general x36, matrix products, local_conv(): jnp.einsum('frkw,kd->frdw', stacked, weight, preferred_element_type=jnp.f...  19 us
    reduce_scatter x1, waiting for transfers between devices, local(): lax.psum_scatter(second_whole, 'dp', scatter_dimension=0, tiled=True)  17.9 us
    unnamed x98, local copies, waits for them, and re-layouts  16.4 us
    ppermute x4, starting transfers between devices, extended_2(): before = lax.ppermute(last, axis, up)  15.3 us
    slice x10, local copies, waits for them, and re-layouts, time_stack(): window[offset:offset + frames]  12.6 us
    slice x22, local copies, waits for them, and re-layouts, local_conv(): weight = kernel[:, tap_row, tap_col].reshape(3 * channels, kernel.shape[4])  9.43 us
    ppermute x4, starting transfers between devices, passed_along(): return lax.ppermute(array, axis, pairs)  8.8 us
  transfers between devices with their start and end apart: 15, of which 4 were waited for; matrix products, arithmetic and copies ran while one was open for 19% of the time, Pallas kernels for 0%

commit v1 on v0

--- a/solution.py
+++ b/solution.py
@@ -1,8 +1,11 @@
+import functools
 import math
 
 import jax
 import jax.numpy as jnp
 from jax import lax
+from jax.experimental import pallas as pl
+from jax.experimental.pallas import tpu as pltpu
 from jax.sharding import PartitionSpec as P
 
 EPSILON = 1e-06
@@ -76,6 +79,148 @@
 
 def flipped(kernel):
     return jnp.swapaxes(kernel[::-1, ::-1, ::-1], 3, 4)
+
+
+def reduce_body(sizes, parts, total, first, wide, narrow_dp, got_dp, narrow_h, got_h, wide_z, got_z, mine, send, recv):
+    dp, heights, depth = sizes
+    tm_index = lax.axis_index("tm")
+    core, level = tm_index % 2, tm_index // 2
+    clip, half = lax.axis_index("dp"), lax.axis_index("height")
+    barrier = pltpu.get_barrier_semaphore()
+    partner = {"tm": level * 2 + 1 - core}
+    clip_peers = [(clip + step) % dp for step in range(1, dp)]
+    half_peers = [(half + step) % heights for step in range(1, heights)]
+    level_peers = [(level + step) % depth for step in range(1, depth)]
+    places = [partner]
+    places += [{"dp": peer} for peer in clip_peers]
+    places += [{"height": peer} for peer in half_peers]
+    places += [{"tm": peer * 2 + core} for peer in level_peers]
+    for place in places:
+        pl.semaphore_signal(barrier, inc=1, device_id=place, device_id_type=pl.DeviceIdType.MESH)
+    pl.semaphore_wait(barrier, len(places))
+    used = [0]
+
+    def send_to(source, target, place):
+        slot = used[0]
+        used[0] += 1
+        copy = pltpu.make_async_remote_copy(
+            src_ref=source,
+            dst_ref=target,
+            send_sem=send.at[slot],
+            recv_sem=recv.at[slot],
+            device_id=place,
+            device_id_type=pl.DeviceIdType.MESH,
+        )
+        copy.start()
+        return copy
+
+    copy = send_to(parts.at[1 - core], first, partner)
+    copy.wait()
+    for index in range(dp):
+        summed = parts[core, index] + first[index]
+        wide[index] = summed
+        narrow_dp[index] = summed.astype(jnp.bfloat16)
+    copies = [
+        send_to(narrow_dp.at[peer], got_dp.at[step], {"dp": peer})
+        for step, peer in enumerate(clip_peers)
+    ]
+    for copy in copies:
+        copy.wait()
+    summed = wide[clip]
+    for step in range(dp - 1):
+        summed = summed + got_dp[step].astype(jnp.float32)
+    wide[0] = summed
+    narrow_h[...] = summed.astype(jnp.bfloat16)
+    copies = [
+        send_to(narrow_h.at[peer], got_h.at[step], {"height": peer})
+        for step, peer in enumerate(half_peers)
+    ]
+    for copy in copies:
+        copy.wait()
+    summed = wide[0, half]
+    for step in range(heights - 1):
+        summed = summed + got_h[step].astype(jnp.float32)
+    wide_z[...] = summed
+    copies = [
+        send_to(wide_z.at[peer], got_z.at[step], {"tm": peer * 2 + core})
+        for step, peer in enumerate(level_peers)
+    ]
+    for copy in copies:
+        copy.wait()
+    summed = wide_z[level]
+    for step in range(depth - 1):
+        summed = summed + got_z[step]
+    mine[core, half, level] = summed.astype(jnp.bfloat16)
+    own = mine.at[core, half, level]
+    copies = [send_to(own, own, {"tm": peer * 2 + core}) for peer in level_peers]
+    for copy in copies:
+        copy.wait()
+    own = mine.at[core, half]
+    copies = [send_to(own, own, {"height": peer}) for peer in half_peers]
+    for copy in copies:
+        copy.wait()
+    own = mine.at[core]
+    copy = send_to(own, own, partner)
+    copy.wait()
+    total[...] = mine[...].astype(jnp.float32)
+
+
+def packed(piece):
+    quarter = piece.shape[0] // 4
+    width = piece.shape[1] // 3
+    rest = piece[3 * quarter :]
+    side = jnp.concatenate([rest[:, i * width : (i + 1) * width] for i in range(3)], axis=0)
+    return jnp.concatenate([piece[: 3 * quarter], side], axis=1)
+
+
+def unpacked(block, channels):
+    quarter = block.shape[0] // 3
+    side = block[:, channels:]
+    rest = jnp.concatenate([side[i * quarter : (i + 1) * quarter] for i in range(3)], axis=1)
+    return jnp.concatenate([block[:, :channels], rest], axis=0)
+
+
+def reduced(terms):
+    dp, heights, depth = (lax.axis_size("dp"), lax.axis_size("height"), lax.axis_size("tm") // 2)
+    channels = terms[0].shape[1]
+    rows = terms[0].shape[0] // dp
+    chunks = []
+    for index in range(dp):
+        chunks.append(
+            jnp.concatenate([packed(term[index * rows : (index + 1) * rows]) for term in terms], axis=0)
+        )
+    pieces = 2 * heights * depth
+    length = chunks[0].shape[0]
+    lanes = chunks[0].shape[1]
+    block = -(-length // (pieces * 16)) * 16
+    stacked = jnp.stack([jnp.pad(chunk, ((0, pieces * block - length), (0, 0))) for chunk in chunks])
+    stacked = stacked.reshape(dp, 2, heights, depth, block, lanes).swapaxes(0, 1)
+    tail = (block, lanes)
+    copies = 2 + (dp - 1) + 2 * (heights - 1) + 2 * (depth - 1)
+    total = pl.pallas_call(
+        functools.partial(reduce_body, (dp, heights, depth)),
+        out_shape=jax.ShapeDtypeStruct((2, heights, depth) + tail, jnp.float32),
+        in_specs=[pl.BlockSpec(memory_space=pltpu.VMEM)],
+        out_specs=pl.BlockSpec(memory_space=pltpu.VMEM),
+        scratch_shapes=[
+            pltpu.VMEM((dp, heights, depth) + tail, jnp.float32),
+            pltpu.VMEM((dp, heights, depth) + tail, jnp.float32),
+            pltpu.VMEM((dp, heights, depth) + tail, jnp.bfloat16),
+            pltpu.VMEM((dp - 1, heights, depth) + tail, jnp.bfloat16),
+            pltpu.VMEM((heights, depth) + tail, jnp.bfloat16),
+            pltpu.VMEM((heights - 1, depth) + tail, jnp.bfloat16),
+            pltpu.VMEM((depth,) + tail, jnp.float32),
+            pltpu.VMEM((depth - 1,) + tail, jnp.float32),
+            pltpu.VMEM((2, heights, depth) + tail, jnp.bfloat16),
+            pltpu.SemaphoreType.DMA((copies,)),
+            pltpu.SemaphoreType.DMA((copies,)),
+        ],
+        compiler_params=pltpu.CompilerParams(collective_id=0, has_side_effects=True),
+        name="reduce_grads",
+    )(stacked)
+    flat = total.reshape(pieces * block, lanes)
+    each = length // len(terms)
+    return [unpacked(flat[i * each : (i + 1) * each], channels) for i in range(len(terms))]
 
 
 def local(clip_input, cotangent, first_kernel, second_kernel):
@@ -117,13 +262,9 @@
         * lax.axis_size("height")
     )
     factor = 1.0 / math.sqrt(positions)
-    first_term = kernel_grad(first_padded, middle_grad, frames) * factor
-    second_term = kernel_grad(second_padded, upstream, frames) * factor
-    first_whole, second_whole = lax.psum((first_term, second_term), ("tm", "height"))
-    first_grad, second_grad = (
-        lax.psum_scatter(first_whole, "dp", scatter_dimension=0, tiled=True),
-        lax.psum_scatter(second_whole, "dp", scatter_dimension=0, tiled=True),
-    )
+    first_term = kernel_grad(first_padded, middle_grad, frames)
+    second_term = kernel_grad(second_padded, upstream, frames)
+    first_grad, second_grad = [whole * factor for whole in reduced((first_term, second_term))]
     return (block_output[None], input_grad[None], first_grad, second_grad)
 
 

time: 242 us -> 171 us (0.71)
  waiting for transfers between devices: 116 us -> 2.21 us
  Pallas kernels: 0 us -> 42.7 us
  between operations: 15 us -> 2.17 us
  local copies, waits for them, and re-layouts: 41.9 us -> 48.8 us
  other arithmetic: 10.3 us -> 17.1 us
    psum x1 -> x0, waiting for transfers between devices: 96.8 us -> none  [local(): lax.psum((first_term, second_term), ('tm', 'height'))]
    pallas_call x0 -> x1, Pallas kernels: none -> 42.7 us  [reduced(): pl.pallas_call(functools.partial(reduce_body, (dp, heights, depth)), out_...]
    reduce_scatter x2 -> x0, waiting for transfers between devices: 17.9 us -> none  [the longest x1 17.9 us: local(): lax.psum_scatter(second_whole, 'dp', scatter_dimension=0, tiled=True)]
    unnamed x98 -> x176, local copies, waits for them, and re-layouts: 16.4 us -> 21.7 us
    slice x0 -> x6, local copies, waits for them, and re-layouts: none -> 3.98 us  [the longest x1 2.12 us: unpacked(): return jnp.concatenate([block[:, :channels], rest], axis=0)]
  transfers between devices with their start and end apart: 15 -> 12, of which waited for: 4 -> 3; matrix products, arithmetic and copies ran while one was open for 19% -> 19% of each run, Pallas kernels for 0% -> 25%
where the time goes in v1:
time: 171 us; the launch traced here: 170 us
  local copies, waits for them, and re-layouts  48.8 us (29%)
  Pallas kernels  42.7 us (25%)
  starting transfers between devices  30 us (18%)
  matrix products  26.7 us (16%)
  other arithmetic  17.1 us (10%)
  waiting for transfers between devices  2.21 us (1%)
  between operations  2.17 us (1%)
    pallas_call x1, Pallas kernels, reduced(): pl.pallas_call(functools.partial(reduce_body, (dp, heights, depth)), out_...  42.7 us
    unnamed x176, local copies, waits for them, and re-layouts  21.7 us
    dot_general x36, matrix products, local_conv(): jnp.einsum('frkw,kd->frdw', stacked, weight, preferred_element_type=jnp.f...  18.5 us
    ppermute x4, starting transfers between devices, extended_2(): before = lax.ppermute(last, axis, up)  16 us
    slice x10, local copies, waits for them, and re-layouts, time_stack(): window[offset:offset + frames]  11.7 us
    slice x22, local copies, waits for them, and re-layouts, local_conv(): weight = kernel[:, tap_row, tap_col].reshape(3 * channels, kernel.shape[4])  9.38 us
    ppermute x4, starting transfers between devices, passed_along(): return lax.ppermute(array, axis, pairs)  8.66 us
    dot_general x18, matrix products, kernel_grad(): jnp.einsum('frkw,frdw->kd', stacked, grad_out, preferred_element_type=jnp...  8.22 us
  transfers between devices with their start and end apart: 12, of which 3 were waited for; matrix products, arithmetic and copies ran while one was open for 19% of the time, Pallas kernels for 25%

profile of v1, /device:TPU:0, one launch (start us, length us, event | category | flops | bytes accessed | tf_op | source)
XLA Modules:
  0.0 169.7 jit_solution(17771686504748833183)
XLA Ops:
  0.6 1.7 slice_bitcast_fusion
  2.3 1.3 collective-permute-start.6
  3.6 1.1 fusion.144
  4.7 1.2 fusion.136
  6.0 3.0 %collective-permute-start = (bf16[2,4,96,128]{3,2,1,0:T(8,128)(2,1)S(1)}, bf16[2,4,96,128]{3,2,1,0:T(8,128)(2,1)S(1)}, u32[]{:S(2)}, u32[]{:S(2)}) collective-permute-start(bf16[2,4,96,128]{3,2,1,0:T(8,128)(2,1)S(1)} %slice.994), channel_id=1, source_target_pairs={{0,2},{2,4},{4,6},{6,8},{8,10},{10,12},{12,14},{1,3},{3,5},{5,7},{... | collective-permute-start | bytes 589832 | tf_op jit(solution)/shard_map/ppermute | solution.py:30
  9.4 0.8 fusion.243
  10.2 1.4 copy.213
  11.7 0.8 fusion.242
  12.6 0.7 copy.257
  13.4 0.7 copy.255
  14.1 0.7 copy.253
  14.8 0.7 copy.251
  15.6 0.7 copy.249
  16.3 0.7 copy.247
  17.0 0.7 copy.245
  17.7 0.7 copy.243
  18.5 0.7 copy.241
  20.3 4.9 %collective-permute-start.7 = (bf16[6,1,96,128]{3,2,1,0:T(8,128)(2,1)S(1)}, bf16[6,1,96,128]{3,2,1,0:T(8,128)(2,1)S(1)}, u32[]{:S(2)}, u32[]{:S(2)}) collective-permute-start(bf16[6,1,96,128]{3,2,1,0:T(8,128)(2,1)S(1)} %get-tuple-element.168), channel_id=1, source_target_pairs={{0,1},{2,3},{4,5},{6,7},{8,9},{10,11},{12,13},{14,15},{16,17},{18,... | collective-permute-start | bytes 442376 | tf_op jit(solution)/shard_map/ppermute | solution.py:21
  25.2 1.3 collective-permute-start.8
  26.6 1.3 collective-permute-start.2
  27.9 4.6 %collective-permute-start.1 = (bf16[6,1,96,128]{3,2,1,0:T(8,128)(2,1)S(1)}, bf16[6,1,96,128]{3,2,1,0:T(8,128)(2,1)S(1)}, u32[]{:S(2)}, u32[]{:S(2)}) collective-permute-start(bf16[6,1,96,128]{3,2,1,0:T(8,128)(2,1)S(1)} %get-tuple-element.177), channel_id=1, source_target_pairs={{0,1},{2,3},{4,5},{6,7},{8,9},{10,11},{12,13},{14,15},{16,17},{18,... | collective-permute-start | bytes 442376 | tf_op jit(solution)/shard_map/ppermute | solution.py:21
  32.5 1.3 collective-permute-done.8
  33.8 1.0 select_maximum_fusion.3
  34.8 2.0 %fusion.223 = (bf16[4,4,96,128]{3,2,1,0:T(8,128)(2,1)S(1)}, bf16[4,4,96,128]{3,2,1,0:T(8,128)(2,1)S(1)}, bf16[4,4,96,128]{3,2,1,0:T(8,128)(2,1)S(1)}, bf16[4,4,9...) fusion(bf16[6,6,96,130]{3,2,1,0:T(8,128)(2,1)S(1)} %select_maxi, ...), kind=kLoop, calls=%fused_computation.355 | loop fusion | bytes 14155776 | tf_op jit(solution)/shard_map/slice | solution.py:47
  36.9 1.0 fusion.8
  37.9 2.1 %fusion.225 = (bf16[4,4,96,128]{3,2,1,0:T(8,128)(2,1)S(1)}, bf16[4,4,96,128]{3,2,1,0:T(8,128)(2,1)S(1)}, bf16[4,4,96,128]{3,2,1,0:T(8,128)(2,1)S(1)}, bf16[4,4,9...) fusion(bf16[6,6,96,130]{3,2,1,0:T(8,128)(2,1)S(1)} %fusion.8), kind=kLoop, calls=%fused_computation.357 | loop fusion | bytes 14155776 | tf_op jit(solution)/shard_map/slice | solution.py:47
  52.5 0.7 multiply_reduce_fusion
  58.1 1.3 collective-permute-start.9
  59.4 3.0 %collective-permute-start.3 = (bf16[2,4,96,128]{3,2,1,0:T(8,128)(2,1)S(1)}, bf16[2,4,96,128]{3,2,1,0:T(8,128)(2,1)S(1)}, u32[]{:S(2)}, u32[]{:S(2)}) collective-permute-start(bf16[2,4,96,128]{3,2,1,0:T(8,128)(2,1)S(1)} %slice.1034), channel_id=1, source_target_pairs={{0,2},{2,4},{4,6},{6,8},{8,10},{10,12},{12,14},{1,3},{3,5},{5,7},{... | collective-permute-start | bytes 589832 | tf_op jit(solution)/shard_map/ppermute | solution.py:30
  62.7 0.7 collective-permute-done.3
  63.5 1.3 collective-permute-start.5
  64.8 4.6 %collective-permute-start.4 = (bf16[6,1,96,128]{3,2,1,0:T(8,128)(2,1)S(1)}, bf16[6,1,96,128]{3,2,1,0:T(8,128)(2,1)S(1)}, u32[]{:S(2)}, u32[]{:S(2)}) collective-permute-start(bf16[6,1,96,128]{3,2,1,0:T(8,128)(2,1)S(1)} %get-tuple-element.173), channel_id=1, source_target_pairs={{0,1},{2,3},{4,5},{6,7},{8,9},{10,11},{12,13},{14,15},{16,17},{18,... | collective-permute-start | bytes 442376 | tf_op jit(solution)/shard_map/ppermute | solution.py:21
  69.4 0.7 fusion.175
  70.1 2.0 %collective-permute-start.10 = (bf16[6,1,96,128]{3,2,1,0:T(8,128)(2,1)}, bf16[6,1,96,128]{3,2,1,0:T(8,128)(2,1)}, u32[]{:S(2)}, u32[]{:S(2)}) collective-permute-start(bf16[6,1,96,128]{3,2,1,0:T(8,128)(2,1)} %get-tuple-element.164), channel_id=1, source_target_pairs={{0,1},{2,3},{4,5},{6,7},{8,9},{10,11},{12,13},{14,15},{16,17},{18,... | collective-permute-start | bytes 442376 | tf_op jit(solution)/shard_map/ppermute | solution.py:21
  72.1 1.5 collective-permute-start.11
  74.4 0.8 fusion.159
  77.2 1.0 select_maximum_fusion.6
  78.2 2.0 %fusion.224 = (bf16[4,4,96,128]{3,2,1,0:T(8,128)(2,1)S(1)}, bf16[4,4,96,128]{3,2,1,0:T(8,128)(2,1)S(1)}, bf16[4,4,96,128]{3,2,1,0:T(8,128)(2,1)S(1)}, bf16[4,4,9...) fusion(bf16[6,6,96,130]{3,2,1,0:T(8,128)(2,1)S(1)} %select_maxi, ...), kind=kLoop, calls=%fused_computation.356 | loop fusion | bytes 14155776 | tf_op jit(solution)/shard_map/slice | solution.py:47
  85.8 1.7 maximum_bitcast_fusion.parts
  87.5 42.7 %reduce_grads.1 = f32[2,2,4,128,128]{4,3,2,1,0:T(8,128)} custom-call(f32[2,2,2,4,128,128]{5,4,3,2,1,0:T(8,128)} %maximum_bitcast_fusion.parts), custom_call_target="tpu_custom_call" | custom-call | tf_op jit(solution)/shard_map/reduce_grads/pallas_call | solution.py:200
  130.2 2.1 %fusion.230 = (f32[972,96]{1,0:T(8,128)}, f32[972,96]{1,0:T(8,128)S(1)}) fusion(f32[2048,128]{1,0:T(8,128)} %bitcast.373), kind=kLoop, calls=%fused_computation.362 | loop fusion | bytes 1492992 | tf_op jit(solution)/shard_map/slice | solution.py:180
  132.3 1.2 fusion.231
  133.5 1.1 pad_maximum_fusion.25
  134.6 1.1 fusion.232
  135.7 1.1 fusion.233
  136.8 1.3 fusion.244
  138.2 1.0 copy.365
  139.2 1.2 copy.364
  140.5 1.0 copy.366
  141.5 1.0 copy.363
  142.5 1.0 copy.362
  143.9 2.0 %select_maximum_fusion = bf16[6,6,96,130]{3,2,1,0:T(8,128)(2,1)S(1)} fusion(bf16[6,1,96,128]{3,2,1,0:T(8,128)(2,1)} %collective-permute-done.11, bf16[6,1,96,128]{3,2,1,0:T(8,128)(2,1)} %collective-permute-done.10, bf16[2,4,96,128]{3,2,1,0:T(8,128)(2,1)S(1)} %collective-permute-done.9, bf16[4,4,96,128]{3,2,1,0:T(8,128)(2,1)S(1)} %get-tuple-element.100), kind=kLoop, calls=%fused_computation.4 | loop fusion | flops 6739200 | bytes 1783296 | tf_op jit(solution)/shard_map/concatenate | solution.py:23
  146.0 2.2 %fusion.222 = (bf16[4,4,96,128]{3,2,1,0:T(8,128)(2,1)S(1)}, bf16[4,4,96,128]{3,2,1,0:T(8,128)(2,1)S(1)}, bf16[4,4,96,128]{3,2,1,0:T(8,128)(2,1)S(1)}, bf16[4,4,9...) fusion(bf16[6,6,96,130]{3,2,1,0:T(8,128)(2,1)S(1)} %select_maxi, ...), kind=kLoop, calls=%fused_computation.354 | loop fusion | bytes 14155776 | tf_op jit(solution)/shard_map/slice | solution.py:47
  151.9 0.5 copy-done.56
  153.8 0.5 copy-done.50
  155.0 0.5 copy-done.2
  155.6 0.7 fusion.145
  160.0 0.5 copy-done.46
  162.2 0.5 copy-done.10
  163.5 0.5 copy-done.40
  165.5 1.3 fusion.16
  166.8 1.1 fusion.143
  167.9 0.9 maximum_multiply_fusion.1
  168.8 0.9 maximum_multiply_fusion
  (283 shorter events, 40.7 us)
Async XLA Ops:
  0.6 8.4 %copy-start.49 = (bf16[2592,96]{0,1:T(8,128)(2,1)S(1)}, bf16[2592,96]{0,1:T(8,128)(2,1)}, u32[]{:S(2)}) copy-start(bf16[2592,96]{0,1:T(8,128)(2,1)} %param.6) | copy-start | bytes 1492996
  2.3 18.0 %collective-permute-start.6 = (bf16[2,4,96,128]{3,2,1,0:T(8,128)(2,1)}, bf16[2,4,96,128]{3,2,1,0:T(8,128)(2,1)S(1)}, u32[]{:S(2)}, u32[]{:S(2)}) collective-permute-start(bf16[2,4,96,128]{3,2,1,0:T(8,128)(2,1)} %slice_bitcast_fusion), channel_id=1, source_target_pairs={{2,0},{4,2},{6,4},{8,6},{10,8},{12,10},{14,12},{3,1},{5,3},{7,5},{... | collective-permute-start | bytes 589832 | tf_op jit(solution)/shard_map/ppermute | solution.py:30
  6.0 20.6 %collective-permute-start = (bf16[2,4,96,128]{3,2,1,0:T(8,128)(2,1)S(1)}, bf16[2,4,96,128]{3,2,1,0:T(8,128)(2,1)S(1)}, u32[]{:S(2)}, u32[]{:S(2)}) collective-permute-start(bf16[2,4,96,128]{3,2,1,0:T(8,128)(2,1)S(1)} %slice.994), channel_id=1, source_target_pairs={{0,2},{2,4},{4,6},{6,8},{8,10},{10,12},{12,14},{1,3},{3,5},{5,7},{... | collective-permute-start | bytes 589832 | tf_op jit(solution)/shard_map/ppermute | solution.py:30
  12.6 7.7 %copy-start = (bf16[1,4,4,96,128]{4,3,2,1,0:T(8,128)(2,1)S(1)}, bf16[1,4,4,96,128]{4,3,2,1,0:T(8,128)(2,1)}, u32[]{:S(2)}) copy-start(bf16[1,4,4,96,128]{4,3,2,1,0:T(8,128)(2,1)} %param.5) | copy-start | bytes 1179652
  20.3 12.2 %collective-permute-start.7 = (bf16[6,1,96,128]{3,2,1,0:T(8,128)(2,1)S(1)}, bf16[6,1,96,128]{3,2,1,0:T(8,128)(2,1)S(1)}, u32[]{:S(2)}, u32[]{:S(2)}) collective-permute-start(bf16[6,1,96,128]{3,2,1,0:T(8,128)(2,1)S(1)} %get-tuple-element.168), channel_id=1, source_target_pairs={{0,1},{2,3},{4,5},{6,7},{8,9},{10,11},{12,13},{14,15},{16,17},{18,... | collective-permute-start | bytes 442376 | tf_op jit(solution)/shard_map/ppermute | solution.py:21
  25.2 8.6 %collective-permute-start.8 = (bf16[6,1,96,128]{3,2,1,0:T(8,128)(2,1)S(1)}, bf16[6,1,96,128]{3,2,1,0:T(8,128)(2,1)S(1)}, u32[]{:S(2)}, u32[]{:S(2)}) collective-permute-start(bf16[6,1,96,128]{3,2,1,0:T(8,128)(2,1)S(1)} %get-tuple-element.169), channel_id=1, source_target_pairs={{1,0},{3,2},{5,4},{7,6},{9,8},{11,10},{13,12},{15,14},{17,16},{19,... | collective-permute-start | bytes 442376 | tf_op jit(solution)/shard_map/ppermute | solution.py:22
  26.6 10.4 %collective-permute-start.2 = (bf16[6,1,96,128]{3,2,1,0:T(8,128)(2,1)S(1)}, bf16[6,1,96,128]{3,2,1,0:T(8,128)(2,1)S(1)}, u32[]{:S(2)}, u32[]{:S(2)}) collective-permute-start(bf16[6,1,96,128]{3,2,1,0:T(8,128)(2,1)S(1)} %get-tuple-element.176), channel_id=1, source_target_pairs={{1,0},{3,2},{5,4},{7,6},{9,8},{11,10},{13,12},{15,14},{17,16},{19,... | collective-permute-start | bytes 442376 | tf_op jit(solution)/shard_map/ppermute | solution.py:22
  27.9 9.1 %collective-permute-start.1 = (bf16[6,1,96,128]{3,2,1,0:T(8,128)(2,1)S(1)}, bf16[6,1,96,128]{3,2,1,0:T(8,128)(2,1)S(1)}, u32[]{:S(2)}, u32[]{:S(2)}) collective-permute-start(bf16[6,1,96,128]{3,2,1,0:T(8,128)(2,1)S(1)} %get-tuple-element.177), channel_id=1, source_target_pairs={{0,1},{2,3},{4,5},{6,7},{8,9},{10,11},{12,13},{14,15},{16,17},{18,... | collective-permute-start | bytes 442376 | tf_op jit(solution)/shard_map/ppermute | solution.py:21
  58.1 11.3 %collective-permute-start.9 = (bf16[2,4,96,128]{3,2,1,0:T(8,128)(2,1)S(1)}, bf16[2,4,96,128]{3,2,1,0:T(8,128)(2,1)S(1)}, u32[]{:S(2)}, u32[]{:S(2)}) collective-permute-start(bf16[2,4,96,128]{3,2,1,0:T(8,128)(2,1)S(1)} %slice.1113), channel_id=1, source_target_pairs={{2,0},{4,2},{6,4},{8,6},{10,8},{12,10},{14,12},{3,1},{5,3},{7,5},{... | collective-permute-start | bytes 589832 | tf_op jit(solution)/shard_map/ppermute | solution.py:30
  59.4 4.1 %collective-permute-start.3 = (bf16[2,4,96,128]{3,2,1,0:T(8,128)(2,1)S(1)}, bf16[2,4,96,128]{3,2,1,0:T(8,128)(2,1)S(1)}, u32[]{:S(2)}, u32[]{:S(2)}) collective-permute-start(bf16[2,4,96,128]{3,2,1,0:T(8,128)(2,1)S(1)} %slice.1034), channel_id=1, source_target_pairs={{0,2},{2,4},{4,6},{6,8},{8,10},{10,12},{12,14},{1,3},{3,5},{5,7},{... | collective-permute-start | bytes 589832 | tf_op jit(solution)/shard_map/ppermute | solution.py:30
  63.5 11.7 %collective-permute-start.5 = (bf16[6,1,96,128]{3,2,1,0:T(8,128)(2,1)S(1)}, bf16[6,1,96,128]{3,2,1,0:T(8,128)(2,1)S(1)}, u32[]{:S(2)}, u32[]{:S(2)}) collective-permute-start(bf16[6,1,96,128]{3,2,1,0:T(8,128)(2,1)S(1)} %get-tuple-element.172), channel_id=1, source_target_pairs={{1,0},{3,2},{5,4},{7,6},{9,8},{11,10},{13,12},{15,14},{17,16},{19,... | collective-permute-start | bytes 442376 | tf_op jit(solution)/shard_map/ppermute | solution.py:22
  64.8 10.4 %collective-permute-start.4 = (bf16[6,1,96,128]{3,2,1,0:T(8,128)(2,1)S(1)}, bf16[6,1,96,128]{3,2,1,0:T(8,128)(2,1)S(1)}, u32[]{:S(2)}, u32[]{:S(2)}) collective-permute-start(bf16[6,1,96,128]{3,2,1,0:T(8,128)(2,1)S(1)} %get-tuple-element.173), channel_id=1, source_target_pairs={{0,1},{2,3},{4,5},{6,7},{8,9},{10,11},{12,13},{14,15},{16,17},{18,... | collective-permute-start | bytes 442376 | tf_op jit(solution)/shard_map/ppermute | solution.py:21
  70.1 63.4 %collective-permute-start.10 = (bf16[6,1,96,128]{3,2,1,0:T(8,128)(2,1)}, bf16[6,1,96,128]{3,2,1,0:T(8,128)(2,1)}, u32[]{:S(2)}, u32[]{:S(2)}) collective-permute-start(bf16[6,1,96,128]{3,2,1,0:T(8,128)(2,1)} %get-tuple-element.164), channel_id=1, source_target_pairs={{0,1},{2,3},{4,5},{6,7},{8,9},{10,11},{12,13},{14,15},{16,17},{18,... | collective-permute-start | bytes 442376 | tf_op jit(solution)/shard_map/ppermute | solution.py:21
  72.1 61.5 %collective-permute-start.11 = (bf16[6,1,96,128]{3,2,1,0:T(8,128)(2,1)}, bf16[6,1,96,128]{3,2,1,0:T(8,128)(2,1)}, u32[]{:S(2)}, u32[]{:S(2)}) collective-permute-start(bf16[6,1,96,128]{3,2,1,0:T(8,128)(2,1)} %get-tuple-element.165), channel_id=1, source_target_pairs={{1,0},{3,2},{5,4},{7,6},{9,8},{11,10},{13,12},{15,14},{17,16},{19,... | collective-permute-start | bytes 442376 | tf_op jit(solution)/shard_map/ppermute | solution.py:22
  80.1 1.0 copy-start.7
  80.2 1.2 copy-start.9
  80.2 1.3 copy-start.11
  80.2 1.4 copy-start.13
  80.2 2.0 %copy-start.15 = (bf16[4,4,96,128]{3,2,1,0:T(8,128)(2,1)}, bf16[4,4,96,128]{3,2,1,0:T(8,128)(2,1)S(1)}, u32[]{:S(2)}) copy-start(bf16[4,4,96,128]{3,2,1,0:T(8,128)(2,1)S(1)} %get-tuple-element.45) | copy-start | bytes 1179652
  80.2 2.0 %copy-start.17 = (bf16[4,4,96,128]{3,2,1,0:T(8,128)(2,1)}, bf16[4,4,96,128]{3,2,1,0:T(8,128)(2,1)S(1)}, u32[]{:S(2)}) copy-start(bf16[4,4,96,128]{3,2,1,0:T(8,128)(2,1)S(1)} %get-tuple-element.46) | copy-start | bytes 1179652
  80.2 2.0 %copy-start.19 = (bf16[4,4,96,128]{3,2,1,0:T(8,128)(2,1)}, bf16[4,4,96,128]{3,2,1,0:T(8,128)(2,1)S(1)}, u32[]{:S(2)}) copy-start(bf16[4,4,96,128]{3,2,1,0:T(8,128)(2,1)S(1)} %get-tuple-element.47) | copy-start | bytes 1179652
  80.2 2.5 %copy-start.21 = (bf16[4,4,96,128]{3,2,1,0:T(8,128)(2,1)}, bf16[4,4,96,128]{3,2,1,0:T(8,128)(2,1)S(1)}, u32[]{:S(2)}) copy-start(bf16[4,4,96,128]{3,2,1,0:T(8,128)(2,1)S(1)} %get-tuple-element.48) | copy-start | bytes 1179652
  80.2 2.5 %copy-start.23 = (bf16[4,4,96,128]{3,2,1,0:T(8,128)(2,1)}, bf16[4,4,96,128]{3,2,1,0:T(8,128)(2,1)S(1)}, u32[]{:S(2)}) copy-start(bf16[4,4,96,128]{3,2,1,0:T(8,128)(2,1)S(1)} %get-tuple-element.49) | copy-start | bytes 1179652
  80.2 2.5 %copy-start.25 = (bf16[4,4,96,128]{3,2,1,0:T(8,128)(2,1)}, bf16[4,4,96,128]{3,2,1,0:T(8,128)(2,1)S(1)}, u32[]{:S(2)}) copy-start(bf16[4,4,96,128]{3,2,1,0:T(8,128)(2,1)S(1)} %get-tuple-element.50) | copy-start | bytes 1179652
  80.2 3.1 %copy-start.27 = (bf16[4,4,96,128]{3,2,1,0:T(8,128)(2,1)}, bf16[4,4,96,128]{3,2,1,0:T(8,128)(2,1)S(1)}, u32[]{:S(2)}) copy-start(bf16[4,4,96,128]{3,2,1,0:T(8,128)(2,1)S(1)} %get-tuple-element.51) | copy-start | bytes 1179652
  80.3 3.1 %copy-start.29 = (bf16[4,4,96,128]{3,2,1,0:T(8,128)(2,1)}, bf16[4,4,96,128]{3,2,1,0:T(8,128)(2,1)S(1)}, u32[]{:S(2)}) copy-start(bf16[4,4,96,128]{3,2,1,0:T(8,128)(2,1)S(1)} %get-tuple-element.52) | copy-start | bytes 1179652
  80.3 3.1 %copy-start.31 = (bf16[4,4,96,128]{3,2,1,0:T(8,128)(2,1)}, bf16[4,4,96,128]{3,2,1,0:T(8,128)(2,1)S(1)}, u32[]{:S(2)}) copy-start(bf16[4,4,96,128]{3,2,1,0:T(8,128)(2,1)S(1)} %get-tuple-element.53) | copy-start | bytes 1179652
  80.3 3.6 %copy-start.33 = (bf16[4,4,96,128]{3,2,1,0:T(8,128)(2,1)}, bf16[4,4,96,128]{3,2,1,0:T(8,128)(2,1)S(1)}, u32[]{:S(2)}) copy-start(bf16[4,4,96,128]{3,2,1,0:T(8,128)(2,1)S(1)} %get-tuple-element.54) | copy-start | bytes 1179652
  80.3 3.6 %copy-start.35 = (bf16[4,4,96,128]{3,2,1,0:T(8,128)(2,1)}, bf16[4,4,96,128]{3,2,1,0:T(8,128)(2,1)S(1)}, u32[]{:S(2)}) copy-start(bf16[4,4,96,128]{3,2,1,0:T(8,128)(2,1)S(1)} %get-tuple-element.55) | copy-start | bytes 1179652
  80.3 3.6 %copy-start.37 = (bf16[4,4,96,128]{3,2,1,0:T(8,128)(2,1)}, bf16[4,4,96,128]{3,2,1,0:T(8,128)(2,1)S(1)}, u32[]{:S(2)}) copy-start(bf16[4,4,96,128]{3,2,1,0:T(8,128)(2,1)S(1)} %get-tuple-element.56) | copy-start | bytes 1179652
  130.1 2.1 %copy-start.1 = (f32[2,2,4,128,128]{4,3,2,1,0:T(8,128)S(1)}, f32[2,2,4,128,128]{4,3,2,1,0:T(8,128)}, u32[]{:S(2)}) copy-start(f32[2,2,4,128,128]{4,3,2,1,0:T(8,128)} %reduce_grads.1) | copy-start | bytes 3145732
  138.2 5.4 %copy-start.48 = (f32[324,32]{1,0:T(8,128)S(1)}, f32[324,32]{1,0:T(8,128)}, u32[]{:S(2)}) copy-start(f32[324,32]{1,0:T(8,128)} %get-tuple-element.98) | copy-start | bytes 124420
  146.0 2.3 %copy-start.53 = (bf16[4,4,96,128]{3,2,1,0:T(8,128)(2,1)S(1)}, bf16[4,4,96,128]{3,2,1,0:T(8,128)(2,1)}, u32[]{:S(2)}) copy-start(bf16[4,4,96,128]{3,2,1,0:T(8,128)(2,1)} %get-tuple-element.105) | copy-start | bytes 1179652
  146.0 2.3 %copy-start.54 = (bf16[4,4,96,128]{3,2,1,0:T(8,128)(2,1)S(1)}, bf16[4,4,96,128]{3,2,1,0:T(8,128)(2,1)}, u32[]{:S(2)}) copy-start(bf16[4,4,96,128]{3,2,1,0:T(8,128)(2,1)} %get-tuple-element.106) | copy-start | bytes 1179652
  146.0 2.3 %copy-start.55 = (bf16[4,4,96,128]{3,2,1,0:T(8,128)(2,1)S(1)}, bf16[4,4,96,128]{3,2,1,0:T(8,128)(2,1)}, u32[]{:S(2)}) copy-start(bf16[4,4,96,128]{3,2,1,0:T(8,128)(2,1)} %get-tuple-element.107) | copy-start | bytes 1179652
  146.0 2.3 %copy-start.65 = (bf16[3,1,1,96,96]{4,3,0,2,1:T(8,128)(2,1)S(1)}, bf16[3,1,1,96,96]{4,3,0,2,1:T(8,128)(2,1)}, u32[]{:S(2)}) copy-start(bf16[3,1,1,96,96]{4,3,0,2,1:T(8,128)(2,1)} %copy.243) | copy-start | bytes 165892
  151.4 1.0 copy-start.60
  153.3 1.1 copy-start.51
  153.3 1.2 copy-start.52
  153.3 1.2 copy-start.58
  154.5 1.0 copy-start.57
  155.5 1.1 copy-start.36
  155.5 1.2 copy-start.38
  155.5 1.5 copy-start.47
  155.6 1.5 copy-start.73
  157.0 1.1 copy-start.30
  157.0 1.2 copy-start.32
  157.0 1.2 copy-start.72
  158.3 1.1 copy-start.24
  158.3 1.2 copy-start.26
  158.3 1.2 copy-start.71
  159.5 1.0 copy-start.70
  160.5 1.1 copy-start.18
  160.5 1.2 copy-start.20
  160.5 1.2 copy-start.69
  161.8 1.1 copy-start.12
  161.8 1.2 copy-start.14
  161.8 1.2 copy-start.68
  163.0 1.1 copy-start.42
  163.0 1.2 copy-start.44
  163.0 1.2 copy-start.67
  164.2 1.1 copy-start.6
  164.2 1.2 copy-start.8
  164.2 1.2 copy-start.66
  (31 other events, 28.4 us)

commit v2 on v0

v2 whole, which is shorter than its diff:
```python
import functools
import math

import jax
import jax.numpy as jnp
from jax import lax
from jax.experimental import pallas as pl
from jax.experimental.pallas import tpu as pltpu
from jax.sharding import PartitionSpec as P

EPSILON = 1e-06
MESH_IDS = pl.DeviceIdType.MESH


def factor_of(value):
    return lax.rsqrt(jnp.mean(value * value, axis=0, keepdims=True) + EPSILON)


def act(value):
    scaled = value * factor_of(value)
    return scaled / (1.0 + jnp.exp(-scaled))


def act_back(value, grad):
    factor = factor_of(value)
    scaled = value * factor
    gate = 1.0 / (1.0 + jnp.exp(-scaled))
    inner = grad * (gate * (1.0 + scaled * (1.0 - gate)))
    return factor * (inner - scaled * jnp.mean(inner * scaled, axis=0, keepdims=True))


def body(
    sizes,
    x,
    cot,
    kernel_one,
    kernel_two,
    flip_one,
    flip_two,
    block_out,
    input_out,
    total,
    acts_one,
    acts_two,
    grads_two,
    grads_one,
    middle,
    second_act,
    middle_grad,
    time_halo,
    row_halo,
    corner_halo,
    terms,
    first,
    wide,
    narrow_dp,
    got_dp,
    narrow_h,
    got_h,
    wide_z,
    got_z,
    mine,
    halo_send,
    halo_recv,
    send,
    recv,
):
    dp, heights, depth = sizes
    frames, rows, channels, cols = x.shape
    shards = 2 * depth
    chunk = terms.shape[1] // dp
    shard = lax.axis_index("tm")
    core, level = shard % 2, shard // 2
    clip, half = lax.axis_index("dp"), lax.axis_index("height")
    other = 1 - half
    has_before, has_after = shard > 0, shard < shards - 1
    edge_row = (rows - 1) * other
    halo_row = (rows + 1) * other
    rim_row = (rows + 1) * half

    barrier = pltpu.get_barrier_semaphore()
    partner = {"tm": level * 2 + 1 - core}
    clip_peers = [(clip + step) % dp for step in range(1, dp)]
    level_peers = [(level + step) % depth for step in range(1, depth)]
    places = [partner, {"height": other}]
    places += [{"dp": peer} for peer in clip_peers]
    places += [{"tm": peer * 2 + core} for peer in level_peers]

    def greet(place):
        pl.semaphore_signal(barrier, inc=1, device_id=place, device_id_type=MESH_IDS)

    for place in places:
        greet(place)

    outer = shard + 2 * core - 1
    has_outer = jnp.logical_and(outer >= 0, outer < shards)

    @pl.when(has_outer)
    def _():
        greet({"tm": outer})

    @pl.when(has_before)
    def _():
        greet({"tm": shard - 1, "height": other})

    @pl.when(has_after)
    def _():
        greet({"tm": shard + 1, "height": other})

    near = has_outer.astype(jnp.int32) + has_before.astype(jnp.int32) + has_after.astype(jnp.int32)
    pl.semaphore_wait(barrier, len(places) + near)

    def remote(source, target, sender, receiver, place):
        return pltpu.make_async_remote_copy(
            src_ref=source,
            dst_ref=target,
            send_sem=sender,
            recv_sem=receiver,
            device_id=place,
            device_id_type=MESH_IDS,
        )

    def exchange(own, slot, ahead):
        step = -1 if ahead else 1
        start = 0 if ahead else frames - 2
        goes, comes = (has_before, has_after) if ahead else (has_after, has_before)
        span = pl.ds(start, 2)
        along = remote(own.at[span], time_halo.at[slot], halo_send.at[slot, 0], halo_recv.at[slot, 0], {"tm": shard + step})
        across = remote(own.at[:, edge_row], row_halo.at[slot], halo_send.at[slot, 1], halo_recv.at[slot, 1], {"height": other})
        corner = remote(
            own.at[span, edge_row],
            corner_halo.at[slot],
            halo_send.at[slot, 2],
            halo_recv.at[slot, 2],
            {"tm": shard + step, "height": other},
        )
        across.start()

        @pl.when(goes)
        def _():
            along.start()
            corner.start()

        def arrive():
            across.wait()

            @pl.when(goes)
            def _():
                along.wait_send()
                corner.wait_send()

            @pl.when(comes)
            def _():
                along.wait_recv()
                corner.wait_recv()

        return arrive

    lane = lax.broadcasted_iota(jnp.int32, (channels, cols), 1)

    def place_tile(field, frame, row, value):
        wide_value = value.astype(jnp.float32)
        left = jnp.where(lane == 0, 0.0, pltpu.roll(wide_value, 1, axis=1))
        right = jnp.where(lane == cols - 1, 0.0, pltpu.roll(wide_value, cols - 1, axis=1))
        field[frame, row, 0:channels] = left.astype(jnp.bfloat16)
        field[frame, row, channels : 2 * channels] = value
        field[frame, row, 2 * channels : 3 * channels] = right.astype(jnp.bfloat16)

    def fill_halo(field, slot, ahead, make):
        inside, outside = (0, frames) if ahead else (2, 0)
        comes = has_after if ahead else has_before
        blank = jnp.zeros((3 * channels, cols), jnp.bfloat16)
        for frame in range(frames + 2):
            field[frame, rim_row] = blank

        def row_step(frame, carry):
            place_tile(field, inside + frame, halo_row, make(row_halo[slot, frame]))
            return carry

        lax.fori_loop(0, frames, row_step, 0)

        @pl.when(comes)
        def _():
            def time_step(index, carry):
                frame, row = index // rows, index % rows
                place_tile(field, outside + frame, row + 1, make(time_halo[slot, frame, row]))
                return carry

            lax.fori_loop(0, 2 * rows, time_step, 0)
            for frame in range(2):
                place_tile(field, outside + frame, halo_row, make(corner_halo[slot, frame]))

        @pl.when(jnp.logical_not(comes))
        def _():
            for frame in range(2):
                for row in range(rows + 2):
                    field[outside + frame, row] = blank

    def conv(field, kernel, finish):
        def step(index, carry):
            frame, row = 2 * (index // rows), index % rows
            summed = None
            for tap in range(3):
                pair = [
                    field[frame + tap + side, pl.ds(row, 3)].reshape(9 * channels, cols) for side in range(2)
                ]
                part = jnp.dot(kernel[tap], jnp.concatenate(pair, axis=1), preferred_element_type=jnp.float32)
                summed = part if summed is None else summed + part
            for side in range(2):
                finish(frame + side, row, summed[:, side * cols : (side + 1) * cols])
            return carry

        lax.fori_loop(0, frames // 2 * rows, step, 0)

    def kernel_grad(slot, field, grad):
        def step(index, carry):
            tap, tap_row = index // 3, index % 3
            tiles = [(frame, row) for frame in range(frames) for row in range(rows)]
            left = jnp.concatenate([field[frame + tap, row + tap_row] for frame, row in tiles], axis=1)
            right = jnp.concatenate([grad[frame, row] for frame, row in tiles], axis=1)
            piece = lax.dot_general(left, right, (((1,), (1,)), ((), ())), preferred_element_type=jnp.float32)
            terms[slot, pl.ds(pl.multiple_of(index * 3 * channels, 3 * channels), 3 * channels)] = piece
            return carry

        lax.fori_loop(0, 9, step, 0)

    def as_act(value):
        return act(value.astype(jnp.float32)).astype(jnp.bfloat16)

    x_arrives = exchange(x, 0, False)
    cot_arrives = exchange(cot, 1, True)

    def first_step(index, carry):
        frame, row = index // rows, index % rows
        place_tile(acts_one, frame + 2, row + 1, as_act(x[frame, row]))
        place_tile(grads_two, frame, row + 1, cot[frame, row])
        return carry

    lax.fori_loop(0, frames * rows, first_step, 0)
    x_arrives()
    fill_halo(acts_one, 0, False, as_act)

    def finish_middle(frame, row, value):
        middle[frame, row] = value
        rounded = act(value).astype(jnp.bfloat16)
        second_act[frame, row] = rounded
        place_tile(acts_two, frame + 2, row + 1, rounded)

    conv(acts_one, kernel_one, finish_middle)
    act_arrives = exchange(second_act, 2, False)
    cot_arrives()
    fill_halo(grads_two, 1, True, lambda value: value)

    def finish_back(frame, row, value):
        rounded = act_back(middle[frame, row], value).astype(jnp.bfloat16)
        middle_grad[frame, row] = rounded
        place_tile(grads_one, frame, row + 1, rounded)

    conv(grads_two, flip_two, finish_back)
    grad_arrives = exchange(middle_grad, 3, True)

    used = [0]

    def send_to(source, target, place):
        slot = used[0]
        used[0] += 1
        copy = remote(source, target, send.at[slot], recv.at[slot], place)
        copy.start()
        return copy

    kernel_grad(0, acts_one, middle_grad)
    act_arrives()
    fill_halo(acts_two, 2, False, lambda value: value)
    kernel_grad(1, acts_two, cot)
    swap = send_to(terms.at[1 - core], first, partner)

    def finish_branch(frame, row, value):
        block_out[frame, row] = x[frame, row].astype(jnp.float32) + value

    def finish_input(frame, row, value):
        back = act_back(x[frame, row].astype(jnp.float32), value)
        input_out[frame, row] = cot[frame, row].astype(jnp.float32) + back

    conv(acts_two, kernel_two, finish_branch)
    swap.wait()
    padded = wide.shape[1]
    for index in range(dp):
        span = pl.ds(index * chunk, chunk)
        summed = terms[core, span] + first[span]
        if padded > chunk:
            summed = jnp.concatenate([summed, jnp.zeros((padded - chunk, channels), jnp.float32)], axis=0)
        wide[index] = summed
        narrow_dp[index] = summed.astype(jnp.bfloat16)
    copies = [send_to(narrow_dp.at[peer], got_dp.at[i], {"dp": peer}) for i, peer in enumerate(clip_peers)]
    grad_arrives()
    fill_halo(grads_one, 3, True, lambda value: value)
    conv(grads_one, flip_one, finish_input)
    for copy in copies:
        copy.wait()
    summed = wide[clip]
    for i in range(dp - 1):
        summed = summed + got_dp[i].astype(jnp.float32)
    wide[0] = summed
    narrow_h[...] = summed.astype(jnp.bfloat16).reshape(narrow_h.shape)
    send_to(narrow_h.at[other], got_h, {"height": other}).wait()
    block = wide_z.shape[1]
    mine_rows = pl.ds(pl.multiple_of(half * (depth * block), depth * block), depth * block)
    summed = wide[0, mine_rows] + got_h[...].astype(jnp.float32)
    wide_z[...] = summed.reshape(wide_z.shape)
    copies = [
        send_to(wide_z.at[peer], got_z.at[i], {"tm": peer * 2 + core}) for i, peer in enumerate(level_peers)
    ]
    for copy in copies:
        copy.wait()
    summed = wide_z[level]
    for i in range(depth - 1):
        summed = summed + got_z[i]
    mine[core, half, level] = summed.astype(jnp.bfloat16)
    own = mine.at[core, half, level]
    copies = [send_to(own, own, {"tm": peer * 2 + core}) for peer in level_peers]
    for copy in copies:
        copy.wait()
    own = mine.at[core, half]
    send_to(own, own, {"height": other}).wait()
    own = mine.at[core]
    send_to(own, own, partner).wait()
    total[...] = mine[...].astype(jnp.float32)


def local(clip_input, cotangent, first_kernel, second_kernel):
    dp, heights, depth = (lax.axis_size("dp"), lax.axis_size("height"), lax.axis_size("tm") // 2)
    assert heights == 2
    _, frames, rows, channels, cols = clip_input.shape
    taps = first_kernel.shape[0]

    def forward(kernel):
        split = kernel.reshape(3, 9 * channels, channels)
        return jnp.swapaxes(split, 1, 2)

    def backward(kernel):
        split = kernel.reshape(3, 3, 3, channels, channels)[::-1, ::-1, ::-1]
        return jnp.transpose(split, (0, 3, 1, 2, 4)).reshape(3, channels, 9 * channels)

    chunk = taps // dp
    block = -(-chunk // (heights * depth * 16)) * 16
    padded = heights * depth * block
    copies = 1 + (dp - 1) + 2 + 2 * (depth - 1) + 1
    tile = (channels, cols)
    field = pltpu.VMEM((frames + 2, rows + 2, 3 * channels, cols), jnp.bfloat16)
    own = (frames, rows) + tile
    vmem = pl.BlockSpec(memory_space=pltpu.VMEM)
    block_output, input_grad, total = pl.pallas_call(
        functools.partial(body, (dp, heights, depth)),
        out_shape=(
            jax.ShapeDtypeStruct(own, jnp.float32),
            jax.ShapeDtypeStruct(own, jnp.float32),
            jax.ShapeDtypeStruct((2, heights, depth, block, channels), jnp.float32),
        ),
        in_specs=[vmem] * 6,
        out_specs=(vmem, vmem, vmem),
        scratch_shapes=[
            field,
            field,
            field,
            field,
            pltpu.VMEM(own, jnp.float32),
            pltpu.VMEM(own, jnp.bfloat16),
            pltpu.VMEM(own, jnp.bfloat16),
            pltpu.VMEM((4, 2, rows) + tile, jnp.bfloat16),
            pltpu.VMEM((4, frames) + tile, jnp.bfloat16),
            pltpu.VMEM((4, 2) + tile, jnp.bfloat16),
            pltpu.VMEM((2, taps, channels), jnp.float32),
            pltpu.VMEM((taps, channels), jnp.float32),
            pltpu.VMEM((dp, padded, channels), jnp.float32),
            pltpu.VMEM((dp, padded, channels), jnp.bfloat16),
            pltpu.VMEM((dp - 1, padded, channels), jnp.bfloat16),
            pltpu.VMEM((heights, depth * block, channels), jnp.bfloat16),
            pltpu.VMEM((depth * block, channels), jnp.bfloat16),
            pltpu.VMEM((depth, block, channels), jnp.float32),
            pltpu.VMEM((depth - 1, block, channels), jnp.float32),
            pltpu.VMEM((2, heights, depth, block, channels), jnp.bfloat16),
            pltpu.SemaphoreType.DMA((4, 3)),
            pltpu.SemaphoreType.DMA((4, 3)),
            pltpu.SemaphoreType.DMA((copies,)),
            pltpu.SemaphoreType.DMA((copies,)),
        ],
        compiler_params=pltpu.CompilerParams(collective_id=0, has_side_effects=True),
        name="block_step",
    )(
        clip_input[0],
        cotangent[0],
        forward(first_kernel),
        forward(second_kernel),
        backward(first_kernel),
        backward(second_kernel),
    )
    positions = frames * rows * cols * dp * heights * lax.axis_size("tm")
    factor = 1.0 / math.sqrt(positions)
    flat = total.reshape(2, padded, channels)[:, :chunk] * factor
    return (block_output[None], input_grad[None], flat[0], flat[1])


def solution(mesh):
    split = P("dp", "tm", "height", None, None)
    return jax.shard_map(
        local,
        mesh=mesh,
        in_specs=(split, split, P(), P()),
        out_specs=(split, split, P("dp", None), P("dp", None)),
        check_vma=False,
    )
```

time: 242 us -> 88.5 us (0.37)
  waiting for transfers between devices: 116 us -> 0 us
  Pallas kernels: 0 us -> 75.9 us
  local copies, waits for them, and re-layouts: 41.9 us -> 11.5 us
  starting transfers between devices: 29.9 us -> 0 us
  matrix products: 27.2 us -> 0 us
  between operations: 15 us -> 0.72 us
  other arithmetic: 10.3 us -> 0.07 us
    psum x1 -> x0, waiting for transfers between devices: 96.8 us -> none  [local(): lax.psum((first_term, second_term), ('tm', 'height'))]
    pallas_call x0 -> x1, Pallas kernels: none -> 75.9 us  [local(): pl.pallas_call(functools.partial(body, (dp, heights, depth)), out_shape=(...]
    ppermute x12 -> x0, starting transfers between devices: 29.5 us -> none  [the longest x4 15.3 us: extended_2(): before = lax.ppermute(last, axis, up)]
    dot_general x54 -> x0, matrix products: 27.2 us -> none  [the longest x36 19 us: local_conv(): jnp.einsum('frkw,kd->frdw', stacked, weight, preferred_element_type=jnp.f...]
    slice x36 -> x1, local copies, waits for them, and re-layouts: 23.1 us -> 1.41 us  [local(): flat = total.reshape(2, padded, channels)[:, :chunk] * factor]
    reduce_scatter x2 -> x0, waiting for transfers between devices: 17.9 us -> none  [the longest x1 17.9 us: local(): lax.psum_scatter(second_whole, 'dp', scatter_dimension=0, tiled=True)]
    unnamed x98 -> x13, local copies, waits for them, and re-layouts: 16.4 us -> 4.33 us
    concatenate x25 -> x0, other arithmetic: 6.05 us -> none  [the longest x8 4.29 us: extended_2(): array = jnp.concatenate([before, array, after], axis=dim)]
  transfers between devices with their start and end apart: 15 -> 0, of which waited for: 4 -> 0; matrix products, arithmetic and copies ran while one was open for 19% -> 0% of each run, Pallas kernels for 0% -> 0%
where the time goes in v2:
time: 88.5 us; the launch traced here: 88.2 us
  Pallas kernels  75.9 us (86%)
  local copies, waits for them, and re-layouts  11.5 us (13%)
    pallas_call x1, Pallas kernels, local(): pl.pallas_call(functools.partial(body, (dp, heights, depth)), out_shape=(...  75.9 us
    unnamed x13, local copies, waits for them, and re-layouts  4.33 us
    reshape x2, local copies, waits for them, and re-layouts, backward(): jnp.transpose(split, (0, 3, 1, 2, 4)).reshape(3, channels, 9 * channels)  2.12 us

profile of v2, /device:TPU:0, one launch (start us, length us, event | category | flops | bytes accessed | tf_op | source)
XLA Modules:
  0.0 88.2 jit_solution(8535940979552109798)
XLA Ops:
  0.6 1.4 %copy.13 = bf16[2592,96]{1,0:T(8,128)(2,1)S(1)} copy(bf16[2592,96]{0,1:T(8,128)(2,1)} %param.6) | data formatting | bytes 995328 | tf_op args[2]
  2.1 0.0 copy-start.1
  2.1 0.3 copy.14
  2.4 1.1 %copy.17.flip_one = bf16[3,96,864]{2,1,0:T(8,128)(2,1)} copy(bf16[3,96,864]{1,2,0:T(8,128)(2,1)S(1)} %bitcast.25) | data formatting | bytes 995328 | tf_op jit(solution)/shard_map/reshape | solution.py:342
  3.5 0.0 copy-done.1
  3.5 0.3 copy.15
  3.8 0.0 copy-start
  3.9 0.3 copy.16
  4.2 1.1 %copy.18.flip_two = bf16[3,96,864]{2,1,0:T(8,128)(2,1)} copy(bf16[3,96,864]{1,2,0:T(8,128)(2,1)S(1)} %bitcast.26) | data formatting | bytes 995328 | tf_op jit(solution)/shard_map/reshape | solution.py:342
  5.3 0.0 copy-done
  5.3 0.4 reshape.29
  5.7 0.4 reshape.30
  6.1 1.1 %copy_bitcast_fusion = (bf16[3,96,864]{2,1,0:T(8,128)(2,1)}, bf16[3,96,864]{2,1,0:T(8,128)(2,1)}) fusion(bf16[3,864,96]{1,0,2:T(4,128)(2,1)S(1)} %reshape.30, bf16[3,864,96]{1,0,2:T(4,128)(2,1)S(1)} %reshape.29), kind=kLoop, calls=%fused_computation.5 | loop fusion | bytes 1990656 | tf_op jit(solution)/shard_map/transpose | solution.py:338
  7.1 75.9 %block_step.1 = (f32[4,4,96,128]{3,2,1,0:T(8,128)}, f32[4,4,96,128]{3,2,1,0:T(8,128)}, f32[2,2,4,176,96]{4,3,2,1,0:T(8,128)}) custom-call(bf16[4,4,96,128]{3,2,1,0:T(8,128)(2,1)} %bitcast.32, bf16[4,4,96,128]{3,2,1,0:T(8,128)(2,1)} %bitcast.33, bf16[3,96,864]{2,1,0:T(8,128)(2,1)} %get-tuple-element.13.kernel_one, ...), custom_call_target="tpu_custom_call" | custom-call | tf_op jit(solution)/shard_map/block_step/pallas_call | solution.py:352
  83.0 1.4 %slice.12 = f32[2,1296,96]{2,1,0:T(8,128)S(1)} slice(f32[2,1408,96]{2,1,0:T(8,128)} %bitcast.29), slice={[0:2], [0:1296], [0:96]} | slice | bytes 1990656 | tf_op jit(solution)/shard_map/slice | solution.py:399
  84.5 0.4 copy.20
  84.9 0.1 broadcast_multiply_fusion
  85.0 0.0 copy-start.3
  85.0 1.0 %slice_bitcast_fusion = (f32[1296,96]{0,1:T(8,128)}, f32[1296,96]{0,1:T(8,128)}) fusion(f32[2,1296,96]{1,2,0:T(8,128)S(1)} %broadcast_multiply_fusion), kind=kLoop, calls=%fused_computation.2 | loop fusion | bytes 1990656 | tf_op jit(solution)/shard_map/squeeze | solution.py:400
  86.0 0.0 copy-start.2
  86.0 0.4 copy-done.3
  86.5 0.9 copy.25
  87.3 0.0 copy-done.2
  87.3 0.9 copy.26
  (2 shorter events, 0.1 us)
Async XLA Ops:
  2.1 1.4 %copy-start.1 = (bf16[2592,96]{0,1:T(8,128)(2,1)S(1)}, bf16[2592,96]{0,1:T(8,128)(2,1)}, u32[]{:S(2)}) copy-start(bf16[2592,96]{0,1:T(8,128)(2,1)} %param.7) | copy-start | bytes 1492996
  3.8 1.4 %copy-start = (bf16[2592,96]{0,1:T(8,128)(2,1)S(1)}, bf16[2592,96]{0,1:T(8,128)(2,1)}, u32[]{:S(2)}) copy-start(bf16[2592,96]{0,1:T(8,128)(2,1)} %param.6) | copy-start | bytes 1492996
  85.0 1.5 %copy-start.3 = (f32[4,4,96,128]{3,2,1,0:T(8,128)S(1)}, f32[4,4,96,128]{3,2,1,0:T(8,128)}, u32[]{:S(2)}) copy-start(f32[4,4,96,128]{3,2,1,0:T(8,128)} %get-tuple-element.7) | copy-start | bytes 2359300
  86.0 1.3 %copy-start.2 = (f32[4,4,96,128]{3,2,1,0:T(8,128)S(1)}, f32[4,4,96,128]{3,2,1,0:T(8,128)}, u32[]{:S(2)}) copy-start(f32[4,4,96,128]{3,2,1,0:T(8,128)} %get-tuple-element.8) | copy-start | bytes 2359300

commit v3 on v2

--- a/solution.py
+++ b/solution.py
@@ -35,11 +35,13 @@
     cot,
     kernel_one,
     kernel_two,
-    flip_one,
-    flip_two,
+    plain_one,
+    plain_two,
     block_out,
     input_out,
     total,
+    flip_one,
+    flip_two,
     acts_one,
     acts_two,
     grads_two,
@@ -58,6 +60,7 @@
     narrow_h,
     got_h,
     wide_z,
+    narrow_z,
     got_z,
     mine,
     halo_send,
@@ -237,6 +240,10 @@
         return carry
 
     lax.fori_loop(0, frames * rows, first_step, 0)
+    for plain, flip in ((plain_two, flip_two), (plain_one, flip_one)):
+        for index in range(27):
+            tile = plain[(26 - index) * channels : (27 - index) * channels]
+            flip[index // 9, :, (index % 9) * channels : (index % 9 + 1) * channels] = tile
     x_arrives()
     fill_halo(acts_one, 0, False, as_act)
 
@@ -307,14 +314,15 @@
     mine_rows = pl.ds(pl.multiple_of(half * (depth * block), depth * block), depth * block)
     summed = wide[0, mine_rows] + got_h[...].astype(jnp.float32)
     wide_z[...] = summed.reshape(wide_z.shape)
+    narrow_z[...] = summed.reshape(wide_z.shape).astype(jnp.bfloat16)
     copies = [
-        send_to(wide_z.at[peer], got_z.at[i], {"tm": peer * 2 + core}) for i, peer in enumerate(level_peers)
+        send_to(narrow_z.at[peer], got_z.at[i], {"tm": peer * 2 + core}) for i, peer in enumerate(level_peers)
     ]
     for copy in copies:
         copy.wait()
     summed = wide_z[level]
     for i in range(depth - 1):
-        summed = summed + got_z[i]
+        summed = summed + got_z[i].astype(jnp.float32)
     mine[core, half, level] = summed.astype(jnp.bfloat16)
     own = mine.at[core, half, level]
     copies = [send_to(own, own, {"tm": peer * 2 + core}) for peer in level_peers]
@@ -336,10 +344,6 @@
     def forward(kernel):
         split = kernel.reshape(3, 9 * channels, channels)
         return jnp.swapaxes(split, 1, 2)
-
-    def backward(kernel):
-        split = kernel.reshape(3, 3, 3, channels, channels)[::-1, ::-1, ::-1]
-        return jnp.transpose(split, (0, 3, 1, 2, 4)).reshape(3, channels, 9 * channels)
 
     chunk = taps // dp
     block = -(-chunk // (heights * depth * 16)) * 16
@@ -359,6 +363,8 @@
         in_specs=[vmem] * 6,
         out_specs=(vmem, vmem, vmem),
         scratch_shapes=[
+            pltpu.VMEM((3, channels, 9 * channels), jnp.bfloat16),
+            pltpu.VMEM((3, channels, 9 * channels), jnp.bfloat16),
             field,
             field,
             field,
@@ -377,7 +383,8 @@
             pltpu.VMEM((heights, depth * block, channels), jnp.bfloat16),
             pltpu.VMEM((depth * block, channels), jnp.bfloat16),
             pltpu.VMEM((depth, block, channels), jnp.float32),
-            pltpu.VMEM((depth - 1, block, channels), jnp.float32),
+            pltpu.VMEM((depth, block, channels), jnp.bfloat16),
+            pltpu.VMEM((depth - 1, block, channels), jnp.bfloat16),
             pltpu.VMEM((2, heights, depth, block, channels), jnp.bfloat16),
             pltpu.SemaphoreType.DMA((4, 3)),
             pltpu.SemaphoreType.DMA((4, 3)),
@@ -391,8 +398,8 @@
         cotangent[0],
         forward(first_kernel),
         forward(second_kernel),
-        backward(first_kernel),
-        backward(second_kernel),
+        first_kernel,
+        second_kernel,
     )
     positions = frames * rows * cols * dp * heights * lax.axis_size("tm")
     factor = 1.0 / math.sqrt(positions)

time: 88.5 us -> 81.1 us (0.916)
  Pallas kernels: 75.9 us -> 69.9 us
  local copies, waits for them, and re-layouts: 11.5 us -> 10.3 us
    pallas_call x1, Pallas kernels: 75.9 us -> 69.9 us  [local(): pl.pallas_call(functools.partial(body, (dp, heights, depth)), out_shape=(...]
    reshape x2 -> x0, local copies, waits for them, and re-layouts: 2.12 us -> none  [backward(): jnp.transpose(split, (0, 3, 1, 2, 4)).reshape(3, channels, 9 * channels)]
    unnamed x13, local copies, waits for them, and re-layouts: 4.33 us -> 5.94 us
where the time goes in v3:
time: 81.1 us; the launch traced here: 80.9 us
  Pallas kernels  69.9 us (86%)
  local copies, waits for them, and re-layouts  10.3 us (13%)
    pallas_call x1, Pallas kernels, local(): pl.pallas_call(functools.partial(body, (dp, heights, depth)), out_shape=(...  69.9 us
    unnamed x13, local copies, waits for them, and re-layouts  5.94 us

profile of v3, /device:TPU:0, one launch (start us, length us, event | category | flops | bytes accessed | tf_op | source)
XLA Modules:
  0.0 80.9 jit_solution(15251834842596198987)
XLA Ops:
  0.6 0.0 copy-start.1
  0.6 0.0 copy-start
  0.7 2.2 %copy.13.plain_one = bf16[2592,96]{1,0:T(8,128)(2,1)} copy(bf16[2592,96]{0,1:T(8,128)(2,1)} %param.6) | data formatting | bytes 995328 | tf_op args[2]
  2.9 0.0 copy-done.1
  2.9 1.1 %copy.14.plain_two = bf16[2592,96]{1,0:T(8,128)(2,1)} copy(bf16[2592,96]{0,1:T(8,128)(2,1)S(1)} %copy-done.1) | data formatting | bytes 995328 | tf_op args[3]
  4.0 0.0 copy-done
  4.0 0.4 reshape.17
  4.4 0.4 reshape.18
  4.8 1.1 %copy_bitcast_fusion = (bf16[3,96,864]{2,1,0:T(8,128)(2,1)}, bf16[3,96,864]{2,1,0:T(8,128)(2,1)}) fusion(bf16[3,864,96]{1,0,2:T(4,128)(2,1)S(1)} %reshape.18, bf16[3,864,96]{1,0,2:T(4,128)(2,1)S(1)} %reshape.17), kind=kLoop, calls=%fused_computation.3 | loop fusion | bytes 1990656 | tf_op jit(solution)/shard_map/transpose | solution.py:346
  5.8 69.9 %block_step.1 = (f32[4,4,96,128]{3,2,1,0:T(8,128)}, f32[4,4,96,128]{3,2,1,0:T(8,128)}, f32[2,2,4,176,96]{4,3,2,1,0:T(8,128)}) custom-call(bf16[4,4,96,128]{3,2,1,0:T(8,128)(2,1)} %bitcast.20, bf16[4,4,96,128]{3,2,1,0:T(8,128)(2,1)} %bitcast.21, bf16[3,96,864]{2,1,0:T(8,128)(2,1)} %get-tuple-element.13.kernel_one, ...), custom_call_target="tpu_custom_call" | custom-call | tf_op jit(solution)/shard_map/block_step/pallas_call | solution.py:356
  75.7 1.4 %slice.12 = f32[2,1296,96]{2,1,0:T(8,128)S(1)} slice(f32[2,1408,96]{2,1,0:T(8,128)} %bitcast.17), slice={[0:2], [0:1296], [0:96]} | slice | bytes 1990656 | tf_op jit(solution)/shard_map/slice | solution.py:406
  77.1 0.4 copy.16
  77.6 0.1 broadcast_multiply_fusion
  77.7 0.0 copy-start.3
  77.7 1.0 %slice_bitcast_fusion = (f32[1296,96]{0,1:T(8,128)}, f32[1296,96]{0,1:T(8,128)}) fusion(f32[2,1296,96]{1,2,0:T(8,128)S(1)} %broadcast_multiply_fusion), kind=kLoop, calls=%fused_computation | loop fusion | bytes 1990656 | tf_op jit(solution)/shard_map/squeeze | solution.py:407
  78.7 0.0 copy-start.2
  78.7 0.4 copy-done.3
  79.1 0.9 %copy.21 = f32[1,4,4,96,128]{4,3,2,1,0:T(8,128)} copy(f32[1,4,4,96,128]{4,3,2,1,0:T(8,128)S(1)} %bitcast.19) | data formatting | bytes 1572864
  80.0 0.0 copy-done.2
  80.0 0.9 %copy.22 = f32[1,4,4,96,128]{4,3,2,1,0:T(8,128)} copy(f32[1,4,4,96,128]{4,3,2,1,0:T(8,128)S(1)} %bitcast.18) | data formatting | bytes 1572864
Async XLA Ops:
  0.6 2.2 %copy-start.1 = (bf16[2592,96]{0,1:T(8,128)(2,1)S(1)}, bf16[2592,96]{0,1:T(8,128)(2,1)}, u32[]{:S(2)}) copy-start(bf16[2592,96]{0,1:T(8,128)(2,1)} %param.7) | copy-start | bytes 1492996
  0.6 3.3 %copy-start = (bf16[2592,96]{0,1:T(8,128)(2,1)S(1)}, bf16[2592,96]{0,1:T(8,128)(2,1)}, u32[]{:S(2)}) copy-start(bf16[2592,96]{0,1:T(8,128)(2,1)} %param.6) | copy-start | bytes 1492996
  77.7 1.5 %copy-start.3 = (f32[4,4,96,128]{3,2,1,0:T(8,128)S(1)}, f32[4,4,96,128]{3,2,1,0:T(8,128)}, u32[]{:S(2)}) copy-start(f32[4,4,96,128]{3,2,1,0:T(8,128)} %get-tuple-element.7) | copy-start | bytes 2359300
  78.7 1.3 %copy-start.2 = (f32[4,4,96,128]{3,2,1,0:T(8,128)S(1)}, f32[4,4,96,128]{3,2,1,0:T(8,128)}, u32[]{:S(2)}) copy-start(f32[4,4,96,128]{3,2,1,0:T(8,128)} %get-tuple-element.8) | copy-start | bytes 2359300

commit v4 on v3

--- a/solution.py
+++ b/solution.py
@@ -199,7 +199,9 @@
                 for row in range(rows + 2):
                     field[outside + frame, row] = blank
 
-    def conv(field, kernel, finish):
+    steps = frames // 2 * rows
+
+    def conv(field, kernel, finish, begin=0, end=steps):
         def step(index, carry):
             frame, row = 2 * (index // rows), index % rows
             summed = None
@@ -213,7 +215,7 @@
                 finish(frame + side, row, summed[:, side * cols : (side + 1) * cols])
             return carry
 
-        lax.fori_loop(0, frames // 2 * rows, step, 0)
+        lax.fori_loop(begin, end, step, 0)
 
     def kernel_grad(slot, field, grad):
         def step(index, carry):
@@ -288,7 +290,7 @@
         back = act_back(x[frame, row].astype(jnp.float32), value)
         input_out[frame, row] = cot[frame, row].astype(jnp.float32) + back
 
-    conv(acts_two, kernel_two, finish_branch)
+    conv(acts_two, kernel_two, finish_branch, 0, steps // 2)
     swap.wait()
     padded = wide.shape[1]
     for index in range(dp):
@@ -299,9 +301,10 @@
         wide[index] = summed
         narrow_dp[index] = summed.astype(jnp.bfloat16)
     copies = [send_to(narrow_dp.at[peer], got_dp.at[i], {"dp": peer}) for i, peer in enumerate(clip_peers)]
+    conv(acts_two, kernel_two, finish_branch, steps // 2, steps)
     grad_arrives()
     fill_halo(grads_one, 3, True, lambda value: value)
-    conv(grads_one, flip_one, finish_input)
+    conv(grads_one, flip_one, finish_input, 0, steps // 2)
     for copy in copies:
         copy.wait()
     summed = wide[clip]
@@ -309,7 +312,9 @@
         summed = summed + got_dp[i].astype(jnp.float32)
     wide[0] = summed
     narrow_h[...] = summed.astype(jnp.bfloat16).reshape(narrow_h.shape)
-    send_to(narrow_h.at[other], got_h, {"height": other}).wait()
+    copy = send_to(narrow_h.at[other], got_h, {"height": other})
+    conv(grads_one, flip_one, finish_input, steps // 2, steps)
+    copy.wait()
     block = wide_z.shape[1]
     mine_rows = pl.ds(pl.multiple_of(half * (depth * block), depth * block), depth * block)
     summed = wide[0, mine_rows] + got_h[...].astype(jnp.float32)

time: 81.1 us -> 80.6 us (level)
  no operation moved by 1% of the time
where the time goes in v4:
time: 80.6 us; the launch traced here: 80.4 us
  Pallas kernels  69.4 us (86%)
  local copies, waits for them, and re-layouts  10.3 us (13%)
    pallas_call x1, Pallas kernels, local(): pl.pallas_call(functools.partial(body, (dp, heights, depth)), out_shape=(...  69.4 us
    unnamed x13, local copies, waits for them, and re-layouts  5.94 us

profile of v4, /device:TPU:0, one launch (start us, length us, event | category | flops | bytes accessed | tf_op | source)
XLA Modules:
  0.0 80.4 jit_solution(13970808356920959905)
XLA Ops:
  0.6 0.0 copy-start.1
  0.6 0.0 copy-start
  0.7 2.2 %copy.13.plain_one = bf16[2592,96]{1,0:T(8,128)(2,1)} copy(bf16[2592,96]{0,1:T(8,128)(2,1)} %param.6) | data formatting | bytes 995328 | tf_op args[2]
  2.9 0.0 copy-done.1
  2.9 1.1 %copy.14.plain_two = bf16[2592,96]{1,0:T(8,128)(2,1)} copy(bf16[2592,96]{0,1:T(8,128)(2,1)S(1)} %copy-done.1) | data formatting | bytes 995328 | tf_op args[3]
  4.0 0.0 copy-done
  4.0 0.4 reshape.17
  4.4 0.4 reshape.18
  4.8 1.1 %copy_bitcast_fusion = (bf16[3,96,864]{2,1,0:T(8,128)(2,1)}, bf16[3,96,864]{2,1,0:T(8,128)(2,1)}) fusion(bf16[3,864,96]{1,0,2:T(4,128)(2,1)S(1)} %reshape.18, bf16[3,864,96]{1,0,2:T(4,128)(2,1)S(1)} %reshape.17), kind=kLoop, calls=%fused_computation.3 | loop fusion | bytes 1990656 | tf_op jit(solution)/shard_map/transpose | solution.py:351
  5.8 69.4 %block_step.1 = (f32[4,4,96,128]{3,2,1,0:T(8,128)}, f32[4,4,96,128]{3,2,1,0:T(8,128)}, f32[2,2,4,176,96]{4,3,2,1,0:T(8,128)}) custom-call(bf16[4,4,96,128]{3,2,1,0:T(8,128)(2,1)} %bitcast.20, bf16[4,4,96,128]{3,2,1,0:T(8,128)(2,1)} %bitcast.21, bf16[3,96,864]{2,1,0:T(8,128)(2,1)} %get-tuple-element.13.kernel_one, ...), custom_call_target="tpu_custom_call" | custom-call | tf_op jit(solution)/shard_map/block_step/pallas_call | solution.py:361
  75.2 1.4 %slice.12 = f32[2,1296,96]{2,1,0:T(8,128)S(1)} slice(f32[2,1408,96]{2,1,0:T(8,128)} %bitcast.17), slice={[0:2], [0:1296], [0:96]} | slice | bytes 1990656 | tf_op jit(solution)/shard_map/slice | solution.py:411
  76.6 0.4 copy.16
  77.1 0.1 broadcast_multiply_fusion
  77.2 0.0 copy-start.3
  77.2 1.0 %slice_bitcast_fusion = (f32[1296,96]{0,1:T(8,128)}, f32[1296,96]{0,1:T(8,128)}) fusion(f32[2,1296,96]{1,2,0:T(8,128)S(1)} %broadcast_multiply_fusion), kind=kLoop, calls=%fused_computation | loop fusion | bytes 1990656 | tf_op jit(solution)/shard_map/squeeze | solution.py:412
  78.2 0.0 copy-start.2
  78.2 0.4 copy-done.3
  78.6 0.9 %copy.21 = f32[1,4,4,96,128]{4,3,2,1,0:T(8,128)} copy(f32[1,4,4,96,128]{4,3,2,1,0:T(8,128)S(1)} %bitcast.19) | data formatting | bytes 1572864
  79.5 0.0 copy-done.2
  79.5 0.9 %copy.22 = f32[1,4,4,96,128]{4,3,2,1,0:T(8,128)} copy(f32[1,4,4,96,128]{4,3,2,1,0:T(8,128)S(1)} %bitcast.18) | data formatting | bytes 1572864
Async XLA Ops:
  0.6 2.2 %copy-start.1 = (bf16[2592,96]{0,1:T(8,128)(2,1)S(1)}, bf16[2592,96]{0,1:T(8,128)(2,1)}, u32[]{:S(2)}) copy-start(bf16[2592,96]{0,1:T(8,128)(2,1)} %param.7) | copy-start | bytes 1492996
  0.6 3.3 %copy-start = (bf16[2592,96]{0,1:T(8,128)(2,1)S(1)}, bf16[2592,96]{0,1:T(8,128)(2,1)}, u32[]{:S(2)}) copy-start(bf16[2592,96]{0,1:T(8,128)(2,1)} %param.6) | copy-start | bytes 1492996
  77.2 1.5 %copy-start.3 = (f32[4,4,96,128]{3,2,1,0:T(8,128)S(1)}, f32[4,4,96,128]{3,2,1,0:T(8,128)}, u32[]{:S(2)}) copy-start(f32[4,4,96,128]{3,2,1,0:T(8,128)} %get-tuple-element.7) | copy-start | bytes 2359300
  78.2 1.3 %copy-start.2 = (f32[4,4,96,128]{3,2,1,0:T(8,128)S(1)}, f32[4,4,96,128]{3,2,1,0:T(8,128)}, u32[]{:S(2)}) copy-start(f32[4,4,96,128]{3,2,1,0:T(8,128)} %get-tuple-element.8) | copy-start | bytes 2359300
